TPU v7x, 32 devices: a whole 2x2x4 slice. The times are simulated.
32 devices in a mesh: row: 4 (over z), col: 8 (over y, x, core).
Axes of the slice: x: 2, y: 2, z: 4, core: 2. Of those that a mesh axis runs over, the one named last changes fastest.
Arguments:
- base_flat: bfloat16 [2, 29568, 8192], P(None, ('row', 'col')), may hold values from -6 to 6
- adjusted_flat: bfloat16 [2, 29568, 8192], P(None, ('row', 'col')), may hold values from -6 to 6
- omega: bfloat16 [2, 8192, 256], P(None, 'col'), may hold values from -6 to 6
Outputs:
- adapter_up_basis: float32 [2, 29568, 256], P(None, ('row', 'col'))
- adapter_down_transposed: float32 [2, 8192, 256], P(None, 'col', 'row')
All inputs are finite; a program needn't handle non-finite values.
Results may differ from a plain program's by a relative error of at most 0.011.
Values may be sent and summed in bfloat16 or wider, within the bound.
No kernel may reach another device: no remote copies, remote signals or barrier semaphores. Data moves between devices by JAX's collectives and lax.ppermute only.
A program may use at most 192 MiB of HBM per device.

v0:
```python
import math

import jax
import jax.numpy as jnp
from jax import lax
from jax.experimental import pallas as pl
from jax.experimental.pallas import tpu as pltpu
from jax.sharding import PartitionSpec as P


HIGHEST = lax.Precision.HIGHEST
STEP = 64
SMALL_KERNEL_BYTES = 12 << 20
PIVOTS = 4
ROW_TILE = 104


def place_on(axis):
    return lax.axis_index(axis).astype(jnp.uint32)


def bit_of(axis, bit):
    return (place_on(axis) >> jnp.uint32(bit.bit_length() - 1)) & jnp.uint32(1)


def swap(value, axis, mask):
    pairs = [(index, index ^ mask) for index in range(lax.axis_size(axis))]
    return lax.ppermute(value, axis, pairs)


def bits_below(size):
    return [1 << place for place in range(size.bit_length() - 1)]


def half_of(value, which, dim):
    half = value.shape[dim] // 2
    return lax.dynamic_slice_in_dim(value, which * jnp.uint32(half), half, dim)


def reduce_half(value, axis, bit, dim):
    mine = bit_of(axis, bit)
    received = swap(half_of(value, mine ^ jnp.uint32(1), dim).astype(jnp.bfloat16), axis, bit)
    return half_of(value, mine, dim).astype(jnp.float32) + received.astype(jnp.float32)


def gather_half(value, axis, bit, dim):
    mine = bit_of(axis, bit)
    received = swap(value, axis, bit)
    low = jnp.where(mine == 0, value, received)
    high = jnp.where(mine == 0, received, value)
    return jnp.concatenate([low, high], axis=dim)


def arrange(parts, place):
    for bit in bits_below(len(parts)):
        odd = (place & jnp.uint32(bit)) != 0
        fresh = list(parts)
        for i in range(len(parts)):
            if not i & bit:
                fresh[i] = jnp.where(odd, parts[i | bit], parts[i])
                fresh[i | bit] = jnp.where(odd, parts[i], parts[i | bit])
        parts = fresh
    return parts


def chip_bits():
    return bits_below(lax.axis_size("col"))[1:]


def reduce_rows(value, dim):
    rows = lax.axis_size("row")
    place = place_on("row")
    size = value.shape[dim] // rows

    def part(owner):
        return lax.dynamic_slice_in_dim(value, owner * jnp.uint32(size), size, dim)

    total = [part(place)]
    for mask in range(1, rows):
        sent = part(place ^ jnp.uint32(mask)).astype(jnp.bfloat16)
        total.append(swap(sent, "row", mask).astype(jnp.float32))
    return tree_sum(total)


def gather_rows(value, dim):
    rows = lax.axis_size("row")
    parts = [value] + [swap(value, "row", mask) for mask in range(1, rows)]
    return jnp.concatenate(arrange(parts, place_on("row")), axis=dim)


def tree_sum(parts):
    while len(parts) > 1:
        parts = [parts[i] + parts[i + 1] for i in range(0, len(parts), 2)]
    return parts[0]


def eliminate(block, row, j):
    columns = [jnp.broadcast_to(block[:, j + i : j + i + 1], block.shape) for i in range(PIVOTS)]
    rows = [block[j + i : j + i + 1, :] for i in range(PIVOTS)]
    corner = [[columns[k][j + i : j + i + 1, :] for k in range(PIVOTS)] for i in range(PIVOTS)]
    for i in range(PIVOTS):
        scale = 1.0 / corner[i][i]
        block = block - jnp.where(row > j + i, columns[i], 0.0) * (rows[i] * scale)
        for k in range(i + 1, PIVOTS):
            ratio = corner[k][i] * scale
            rows[k] = rows[k] - ratio * rows[i]
            columns[k] = columns[k] - columns[i] * ratio
            for l in range(k, PIVOTS):
                corner[l][k] = corner[l][k] - corner[l][i] * ratio
    return block


def inverse_factor_kernel(gram_ref, inverse_ref, work_ref):
    count, rank, _ = gram_ref.shape
    step = min(STEP, rank)
    row = lax.broadcasted_iota(jnp.int32, (step, 2 * step), 0)
    lane = lax.broadcasted_iota(jnp.int32, (step, 2 * step), 1)
    eye = jnp.where(lane == row + step, 1.0, 0.0)[:, step:]
    full = lax.broadcasted_iota(jnp.int32, (step, rank), 1)
    for m in range(count):
        work_ref[m] = gram_ref[m]
    for start in range(0, rank, step):
        stop = start + step
        blocks = [
            jnp.concatenate([work_ref[m, start:stop, start:stop], eye], axis=1)
            for m in range(count)
        ]
        for j in range(0, step, PIVOTS):
            for m in range(count):
                blocks[m] = eliminate(blocks[m], row, j)
        for m in range(count):
            block = blocks[m]
            diagonal = jnp.sum(jnp.where(lane == row, block, 0.0), axis=1, keepdims=True)
            inverse = block[:, step:] * lax.rsqrt(diagonal)
            unit = [jnp.zeros((step, start), jnp.float32)] if start else []
            unit += [eye]
            unit += [jnp.zeros((step, rank - stop), jnp.float32)] if stop < rank else []
            unit = jnp.concatenate(unit, axis=1) if len(unit) > 1 else unit[0]
            panel = jnp.where((full >= start) & (full < stop), unit, work_ref[m, start:stop, :])
            solved = jnp.dot(inverse, panel, precision=HIGHEST, preferred_element_type=jnp.float32)
            inverse_ref[m, start:stop, :] = jnp.where(full < stop, solved, 0.0)
            if stop < rank:
                rest = work_ref[m, stop:, :]
                wide = lax.broadcasted_iota(jnp.int32, rest.shape, 1)
                rest = jnp.where((wide >= start) & (wide < stop), 0.0, rest)
                work_ref[m, stop:, :] = rest - lax.dot_general(
                    solved[:, stop:],
                    solved,
                    (((0,), (0,)), ((), ())),
                    precision=HIGHEST,
                    preferred_element_type=jnp.float32,
                )


def inverse_factor(gram):
    return pl.pallas_call(
        inverse_factor_kernel,
        out_shape=jax.ShapeDtypeStruct(gram.shape, jnp.float32),
        scratch_shapes=[pltpu.VMEM(gram.shape, jnp.float32)],
        compiler_params=pltpu.CompilerParams(vmem_limit_bytes=SMALL_KERNEL_BYTES),
        name="inverse_factor",
    )(gram)


def sum_everywhere(gram):
    columns = lax.axis_size("col")
    rows = lax.axis_size("row")
    chips = columns // 2
    mine = bit_of("col", 1)
    chip = place_on("col") >> jnp.uint32(1)
    value = half_of(gram, mine, 1) + swap(half_of(gram, mine ^ jnp.uint32(1), 1), "col", 1)
    chunk = value.shape[1] // chips

    def part(owner):
        return lax.dynamic_slice_in_dim(value, owner * jnp.uint32(chunk), chunk, 1)

    parts = [part(chip)]
    for mask in range(1, chips):
        parts.append(swap(part(chip ^ jnp.uint32(mask)), "col", 2 * mask))
    value = tree_sum(parts)
    value = tree_sum([value] + [swap(value, "row", mask) for mask in range(1, rows)])
    parts = [value] + [swap(value, "col", 2 * mask) for mask in range(1, chips)]
    whole = jnp.concatenate(arrange(parts, chip), axis=1)
    return gather_half(whole, "col", 1, 1)


def product(left, right, dims):
    dims = ((dims[:1], dims[1:]), ((), ()))
    return lax.dot_general(left, right, dims, precision=HIGHEST, preferred_element_type=jnp.float32)


def factors(panels):
    grams = jnp.stack([product(panel, panel, (0, 0)) for panel in panels])
    return inverse_factor(sum_everywhere(grams))


def difference_kernel(adjusted_ref, base_ref, *delta_refs):
    wide = adjusted_ref[...].astype(jnp.float32) - base_ref[...].astype(jnp.float32)
    wide = jnp.swapaxes(wide, 0, 1)
    for m, delta_ref in enumerate(delta_refs):
        delta_ref[...] = wide[m].astype(jnp.bfloat16)


def differences(adjusted, base):
    matrices, rows, width = base.shape
    tall = min(ROW_TILE, rows)
    stacked = pl.BlockSpec((tall, matrices, width), lambda i: (i, 0, 0))
    return pl.pallas_call(
        difference_kernel,
        out_shape=(jax.ShapeDtypeStruct((rows, width), jnp.bfloat16),) * matrices,
        grid=(pl.cdiv(rows, tall),),
        in_specs=[stacked, stacked],
        out_specs=(pl.BlockSpec((tall, width), lambda i: (i, 0)),) * matrices,
        name="difference",
    )(adjusted.transpose(1, 0, 2), base.transpose(1, 0, 2))


def assemble_kernel(place_ref, *refs):
    *part_refs, out_ref, sems = refs
    length = part_refs[0].shape[0]
    copies = []
    for index, part_ref in enumerate(part_refs):
        start = pl.multiple_of((place_ref[0] ^ index) * length, length)
        copies.append(pltpu.make_async_copy(part_ref, out_ref.at[pl.ds(start, length), :], sems.at[index]))
    for copy in copies:
        copy.start()
    for copy in copies:
        copy.wait()


def assemble(parts, place):
    length, rank = parts[0].shape
    return pl.pallas_call(
        assemble_kernel,
        out_shape=jax.ShapeDtypeStruct((len(parts) * length, rank), parts[0].dtype),
        in_specs=[pl.BlockSpec(memory_space=pltpu.SMEM)]
        + [pl.BlockSpec(memory_space=pl.ANY)] * len(parts),
        out_specs=pl.BlockSpec(memory_space=pltpu.VMEM),
        scratch_shapes=[pltpu.SemaphoreType.DMA((len(parts),))],
        compiler_params=pltpu.CompilerParams(vmem_limit_bytes=SMALL_KERNEL_BYTES),
        name="assemble",
    )(place[None], *parts)


def forward(delta, right):
    return jnp.dot(delta, right, preferred_element_type=jnp.float32)


def backward(delta, basis):
    total = lax.dot_general(delta, basis, (((0,), (0,)), ((), ())), preferred_element_type=jnp.float32)
    return total.astype(jnp.bfloat16)


def near_parts(share):
    return [share] + [swap(share, "col", mask) for mask in range(2, lax.axis_size("col"), 2)]


def with_other_core(near):
    parts = []
    for part in near:
        parts += [part, swap(part, "col", 1)]
    return parts


def reduce_chips(shares_of, leading):
    bits = chip_bits()

    def step(share, order, turn):
        if not leading:
            return reduce_half(share, "col", order[turn], 0)
        left = sorted(order[turn:], reverse=True)
        dim = left.index(order[turn])
        return lax.squeeze(reduce_half(share, "col", order[turn], dim), (dim,))

    orders = (bits, bits[::-1])
    for m, shares in enumerate(shares_of):
        for turn in range(len(bits)):
            fresh = []
            for share, order in zip(shares, orders):
                fresh.append(step(share, order, turn))
            shares = fresh
        shares_of[m] = shares
    return shares_of


def core_sum(delta, basis):
    bits = chip_bits()
    total = lax.optimization_barrier(backward(delta, basis))
    width = total.shape[0] // lax.axis_size("col")
    total = total.reshape((2,) * len(bits) + (2, width, total.shape[1]))
    return lax.squeeze(reduce_half(total, "col", 1, len(bits)), (len(bits),))


def two_shares(total, dim):
    half = total.shape[dim] // 2
    return [lax.slice_in_dim(total, start, start + half, axis=dim) for start in (0, half)]


def all_columns(deltas, bases):
    bits = chip_bits()
    totals = [reduce_half(backward(delta, basis), "col", 1, 0) for delta, basis in zip(deltas, bases)]
    columns = []
    for shares in reduce_chips([two_shares(total, 0) for total in totals], False):
        value = gather_rows(reduce_rows(jnp.stack(shares), 1).astype(jnp.bfloat16), 1)
        shares = []
        for index, order in ((0, bits[::-1]), (1, bits)):
            share = value[index]
            for bit in order:
                share = gather_half(share, "col", bit, 0)
            shares.append(share)
        columns.append(gather_half(jnp.concatenate(shares, axis=0), "col", 1, 0))
    return columns


def transposed_kernel(*refs):
    out_ref, start = refs[-1], 0
    for ref in refs[:-1]:
        out_ref[:, start : start + ref.shape[0]] = ref[...].T
        start += ref.shape[0]


def transposed(pieces):
    length = sum(piece.shape[0] for piece in pieces)
    return pl.pallas_call(
        transposed_kernel,
        out_shape=jax.ShapeDtypeStruct((pieces[0].shape[1], length), jnp.float32),
        compiler_params=pltpu.CompilerParams(vmem_limit_bytes=SMALL_KERNEL_BYTES),
        name="transposed",
    )(*pieces)


def own_downs(deltas, bases):
    totals = [core_sum(delta, basis.astype(jnp.bfloat16)) for delta, basis in zip(deltas, bases)]
    bases, totals[-1] = lax.optimization_barrier((bases, totals[-1]))
    shares_of = reduce_chips([two_shares(total, total.ndim - 2) for total in totals], True)
    return [reduce_rows(transposed(shares), 0) for shares in shares_of], bases


def extract(base_flat, adjusted_flat, omega):
    matrices, _, _ = omega.shape
    hidden_units = base_flat.shape[1] * lax.axis_size("row") * lax.axis_size("col")
    every = range(matrices)
    near = [near_parts(omega[m]) for m in every]
    deltas = differences(adjusted_flat, base_flat)
    deltas, near = lax.optimization_barrier((deltas, near))
    place = lax.axis_index("col")
    panels = [forward(deltas[m], assemble(with_other_core(near[m]), place)) for m in every]
    inverses = factors(panels)
    first = [product(panels[m], inverses[m], (1, 1)).astype(jnp.bfloat16) for m in every]
    columns = all_columns(deltas, first)
    panels = [forward(deltas[m], columns[m]) for m in every]
    inverses = factors(panels)
    last = [product(panels[m], inverses[m], (1, 1)) for m in every]
    downs, last = own_downs(deltas, last)
    down = jnp.stack(downs).transpose(0, 2, 1)
    up = jnp.stack([math.sqrt(hidden_units) * last[m] for m in every])
    return (up, down)


def solution(mesh):
    in_specs = (P(None, ("row", "col"), None), P(None, ("row", "col"), None), P(None, "col", None))
    out_specs = (P(None, ("row", "col"), None), P(None, "col", "row"))
    return jax.shard_map(extract, mesh=mesh, in_specs=in_specs, out_specs=out_specs, check_vma=False)
```

profile of v0, /device:TPU:0, one launch (start us, length us, event | category | flops | bytes accessed | tf_op | source)
XLA Modules:
  0.0 408.2 jit_solution(10974430649993944996)
XLA Ops:
  1.9 4.0 collective-permute-start.5
  6.5 2.8 collective-permute-start.2
  9.9 8.8 %collective-permute-done.5.refs_6_ = bf16[1024,256]{1,0:T(8,128)(2,1)S(1)} collective-permute-done((bf16[1024,256]{1,0:T(8,128)(2,1)S(1)}, bf16[1024,256]{1,0:T(8,128)(2,1)S(1)}, u32[]{:S(2)}, u32[]{:S(2)}) %collective-permute-start.5) | collective-permute-done | bytes 524320 | tf_op jit(solution)/shard_map/ppermute | solution.py:28
  20.7 35.4 %difference.1 = (bf16[924,8192]{1,0:T(8,128)(2,1)}, bf16[924,8192]{1,0:T(8,128)(2,1)}) custom-call(bf16[924,2,8192]{2,1,0:T(2,128)(2,1)} %bitcast.139, bf16[924,2,8192]{2,1,0:T(2,128)(2,1)} %bitcast.140), custom_call_target="tpu_custom_call" | custom-call | tf_op jit(solution)/shard_map/difference/pallas_call | solution.py:208
  62.5 7.8 %fusion.52 = f32[924,256]{1,0:T(8,128)S(1)} fusion(bf16[924,8192]{1,0:T(8,128)(2,1)} %get-tuple-element.19, bf16[8192,256]{1,0:T(8,128)(2,1)S(1)} %assemble.2), kind=kOutput, calls=%fused_computation.226 | convolution fusion | flops 3875536896 | bytes 20279296 | tf_op jit(solution)/shard_map/dot_general | solution.py:246
  73.1 4.1 fusion.53
  80.9 2.9 collective-permute-start.17
  85.4 2.0 collective-permute-done.17
  88.3 3.7 collective-permute-start.20
  92.7 2.4 collective-permute-done.20
  95.2 2.3 collective-permute-done.19
  98.7 2.3 collective-permute-start.21
  101.9 2.1 collective-permute-done.22
  105.7 12.4 %inverse_factor.2 = f32[2,256,256]{2,1,0:T(8,128)S(1)} custom-call(f32[2,256,256]{2,1,0:T(8,128)S(1)} %pad_maximum_fusion.3.gram_ref), custom_call_target="tpu_custom_call" | custom-call | tf_op jit(solution)/shard_map/inverse_factor/pallas_call | solution.py:156
  119.1 10.3 %convolution_convert_fusion.3 = bf16[8192,256]{1,0:T(8,128)(2,1)S(1)} fusion(bf16[924,8192]{1,0:T(8,128)(2,1)} %get-tuple-element.19, bf16[924,256]{1,0:T(8,128)(2,1)S(1)} %convolution_convert_fusion.5), kind=kOutput, calls=%fused_computation.3 | convolution fusion | flops 3877634048 | bytes 19806208 | tf_op jit(solution)/shard_map/dot_general | solution.py:250
  133.2 5.6 %convolution_convert_fusion.2 = bf16[8192,256]{1,0:T(8,128)(2,1)S(1)} fusion(bf16[924,8192]{1,0:T(8,128)(2,1)S(1)} %bitcast.148, bf16[924,256]{1,0:T(8,128)(2,1)S(1)} %convolution_convert_fusion.4), kind=kOutput, calls=%fused_computation.2 | convolution fusion | flops 3877634048 | bytes 19806208 | tf_op jit(solution)/shard_map/dot_general | solution.py:250
  141.1 2.7 convert_add_fusion.1
  147.2 2.0 convert_add_fusion
  151.4 7.6 %collective-permute-done.26 = bf16[1024,256]{1,0:T(8,128)(2,1)S(1)} collective-permute-done((bf16[1024,256]{1,0:T(8,128)(2,1)S(1)}, bf16[1024,256]{1,0:T(8,128)(2,1)S(1)}, u32[]{:S(2)}, u32[]{:S(2)}) %collective-permute-start.26) | collective-permute-done | bytes 524320 | tf_op jit(solution)/shard_map/ppermute | solution.py:28
  162.3 7.9 %collective-permute-done.42 = bf16[1024,256]{1,0:T(8,128)(2,1)S(1)} collective-permute-done((bf16[1024,256]{1,0:T(8,128)(2,1)S(1)}, bf16[1024,256]{1,0:T(8,128)(2,1)S(1)}, u32[]{:S(2)}, u32[]{:S(2)}) %collective-permute-start.42) | collective-permute-done | bytes 524320 | tf_op jit(solution)/shard_map/ppermute | solution.py:28
  173.6 4.2 %collective-permute-done.27 = bf16[512,256]{1,0:T(8,128)(2,1)S(1)} collective-permute-done((bf16[512,256]{1,0:T(8,128)(2,1)S(1)}, bf16[512,256]{1,0:T(8,128)(2,1)S(1)}, u32[]{:S(2)}, u32[]{:S(2)}) %collective-permute-start.27) | collective-permute-done | bytes 262176 | tf_op jit(solution)/shard_map/ppermute | solution.py:28
  179.1 2.2 collective-permute-start.31
  183.2 7.3 %collective-permute-done.31 = bf16[2,128,256]{2,1,0:T(8,128)(2,1)S(1)} collective-permute-done((bf16[2,128,256]{2,1,0:T(8,128)(2,1)S(1)}, bf16[2,128,256]{2,1,0:T(8,128)(2,1)S(1)}, u32[]{:S(2)}, u32[]{:S(2)}) %collective-permute-start.31) | collective-permute-done | bytes 131104 | tf_op jit(solution)/shard_map/ppermute | solution.py:28
  190.6 2.0 collective-permute-start.35
  201.5 4.1 %collective-permute-done.34 = bf16[2,128,256]{2,1,0:T(8,128)(2,1)S(1)} collective-permute-done((bf16[2,128,256]{2,1,0:T(8,128)(2,1)S(1)}, bf16[2,128,256]{2,1,0:T(8,128)(2,1)S(1)}, u32[]{:S(2)}, u32[]{:S(2)}) %collective-permute-start.34) | collective-permute-done | bytes 131104 | tf_op jit(solution)/shard_map/ppermute | solution.py:28
  207.8 7.2 %collective-permute-done.47 = bf16[2,128,256]{2,1,0:T(8,128)(2,1)S(1)} collective-permute-done((bf16[2,128,256]{2,1,0:T(8,128)(2,1)S(1)}, bf16[2,128,256]{2,1,0:T(8,128)(2,1)S(1)}, u32[]{:S(2)}, u32[]{:S(2)}) %collective-permute-start.47) | collective-permute-done | bytes 131104 | tf_op jit(solution)/shard_map/ppermute | solution.py:28
  215.1 2.3 collective-permute-start.51
  221.3 7.8 %collective-permute-done.50 = bf16[2,128,256]{2,1,0:T(8,128)(2,1)S(1)} collective-permute-done((bf16[2,128,256]{2,1,0:T(8,128)(2,1)S(1)}, bf16[2,128,256]{2,1,0:T(8,128)(2,1)S(1)}, u32[]{:S(2)}, u32[]{:S(2)}) %collective-permute-start.50) | collective-permute-done | bytes 131104 | tf_op jit(solution)/shard_map/ppermute | solution.py:28
  233.0 11.0 %collective-permute-done.37 = bf16[1024,256]{1,0:T(8,128)(2,1)S(1)} collective-permute-done((bf16[1024,256]{1,0:T(8,128)(2,1)S(1)}, bf16[1024,256]{1,0:T(8,128)(2,1)S(1)}, u32[]{:S(2)}, u32[]{:S(2)}) %collective-permute-start.37) | collective-permute-done | bytes 524320 | tf_op jit(solution)/shard_map/ppermute | solution.py:28
  244.4 2.5 collective-permute-done.54
  249.0 9.9 %collective-permute-done.55 = bf16[1024,256]{1,0:T(8,128)(2,1)S(1)} collective-permute-done((bf16[1024,256]{1,0:T(8,128)(2,1)S(1)}, bf16[1024,256]{1,0:T(8,128)(2,1)S(1)}, u32[]{:S(2)}, u32[]{:S(2)}) %collective-permute-start.55) | collective-permute-done | bytes 524320 | tf_op jit(solution)/shard_map/ppermute | solution.py:28
  260.4 7.5 %fusion = f32[924,256]{1,0:T(8,128)S(1)} fusion(bf16[924,8192]{1,0:T(8,128)(2,1)} %get-tuple-element.19, bf16[4096,256]{1,0:T(8,128)(2,1)S(1)} %get-tuple-element.45, bf16[4096,256]{1,0:T(8,128)(2,1)S(1)} %get-tuple-element.44), kind=kOutput, calls=%fused_computation.4 | convolution fusion | flops 3883925504 | bytes 20279296 | tf_op jit(solution)/shard_map/dot_general | solution.py:246
  270.6 7.6 %fusion.4 = f32[924,256]{1,0:T(8,128)S(1)} fusion(bf16[924,8192]{1,0:T(8,128)(2,1)} %get-tuple-element.24, bf16[4096,256]{1,0:T(8,128)(2,1)S(1)} %get-tuple-element.41, bf16[4096,256]{1,0:T(8,128)(2,1)S(1)} %get-tuple-element.40), kind=kOutput, calls=%fused_computation.8 | convolution fusion | flops 3883925504 | bytes 20279296 | tf_op jit(solution)/shard_map/dot_general | solution.py:246
  286.4 2.6 collective-permute-done.60
  291.3 4.4 %collective-permute-start.62 = (f32[2,32,256]{2,1,0:T(8,128)S(1)}, f32[2,32,256]{2,1,0:T(8,128)S(1)}, u32[]{:S(2)}, u32[]{:S(2)}) collective-permute-start(f32[2,32,256]{2,1,0:T(8,128)S(1)} %add_add_fusion.1), channel_id=1, source_target_pairs={{0,16},{8,24},{16,0},{24,8},{1,17},{9,25},{17,1},{25,9},{2,18},{10... | collective-permute-start | bytes 196616 | tf_op jit(solution)/shard_map/ppermute | solution.py:28
  296.3 4.3 %collective-permute-done.62 = f32[2,32,256]{2,1,0:T(8,128)S(1)} collective-permute-done((f32[2,32,256]{2,1,0:T(8,128)S(1)}, f32[2,32,256]{2,1,0:T(8,128)S(1)}, u32[]{:S(2)}, u32[]{:S(2)}) %collective-permute-start.62) | collective-permute-done | bytes 65568 | tf_op jit(solution)/shard_map/ppermute | solution.py:28
  309.8 12.3 %inverse_factor.3 = f32[2,256,256]{2,1,0:T(8,128)S(1)} custom-call(f32[2,256,256]{2,1,0:T(8,128)S(1)} %pad_maximum_fusion.10.gram_ref), custom_call_target="tpu_custom_call" | custom-call | tf_op jit(solution)/shard_map/inverse_factor/pallas_call | solution.py:156
  324.3 10.2 %convolution_convert_fusion = bf16[8192,256]{1,0:T(8,128)(2,1)S(1)} fusion(bf16[924,8192]{1,0:T(8,128)(2,1)} %get-tuple-element.19, f32[924,256]{1,0:T(8,128)S(1)} %fusion.45), kind=kOutput, calls=%fused_computation | convolution fusion | flops 3877870592 | bytes 20279296 | tf_op jit(solution)/shard_map/dot_general | solution.py:250
  337.3 5.5 %convolution_convert_fusion.1 = bf16[8192,256]{1,0:T(8,128)(2,1)S(1)} fusion(bf16[924,8192]{1,0:T(8,128)(2,1)S(1)} %bitcast.150, f32[924,256]{1,0:T(8,128)S(1)} %fusion.44), kind=kOutput, calls=%fused_computation.1 | convolution fusion | flops 3877870592 | bytes 20279296 | tf_op jit(solution)/shard_map/dot_general | solution.py:250
  342.9 2.0 copy-done.5
  346.8 2.7 add_bitcast_fusion
  352.1 2.0 add_bitcast_fusion.1
  354.7 2.7 copy.10
  359.6 5.1 %collective-permute-done.70 = bf16[2,1,512,256]{3,2,1,0:T(8,128)(2,1)S(1)} collective-permute-done((bf16[2,1,512,256]{3,2,1,0:T(8,128)(2,1)S(1)}, bf16[2,1,512,256]{3,2,1,0:T(8,128)(2,1)S(1)}, u32[]{:S(2)}, u32[]{:S(2)}) %collective-permute-start.70) | collective-permute-done | bytes 524320 | tf_op jit(solution)/shard_map/ppermute | solution.py:28
  367.2 8.8 %collective-permute-done.77 = bf16[2,1,512,256]{3,2,1,0:T(8,128)(2,1)S(1)} collective-permute-done((bf16[2,1,512,256]{3,2,1,0:T(8,128)(2,1)S(1)}, bf16[2,1,512,256]{3,2,1,0:T(8,128)(2,1)S(1)}, u32[]{:S(2)}, u32[]{:S(2)}) %collective-permute-start.77) | collective-permute-done | bytes 524320 | tf_op jit(solution)/shard_map/ppermute | solution.py:28
  378.4 4.0 collective-permute-done.71
  391.8 11.2 %collective-permute-done.75 = bf16[64,1024]{1,0:T(8,128)(2,1)S(1)} collective-permute-done((bf16[64,1024]{1,0:T(8,128)(2,1)S(1)}, bf16[64,1024]{1,0:T(8,128)(2,1)S(1)}, u32[]{:S(2)}, u32[]{:S(2)}) %collective-permute-start.75) | collective-permute-done | bytes 131104 | tf_op jit(solution)/shard_map/ppermute | solution.py:28
  403.1 4.0 collective-permute-done.82
  (281 shorter events, 119.5 us)
Async XLA Ops:
  1.9 16.8 %collective-permute-start.5 = (bf16[1024,256]{1,0:T(8,128)(2,1)S(1)}, bf16[1024,256]{1,0:T(8,128)(2,1)S(1)}, u32[]{:S(2)}, u32[]{:S(2)}) collective-permute-start(bf16[1024,256]{1,0:T(8,128)(2,1)S(1)} %get-tuple-element.25.refs_0_), channel_id=1, source_target_pairs={{0,6},{1,7},{2,4},{3,5},{4,2},{5,3},{6,0},{7,1},{8,14},{9,15},{10,... | collective-permute-start | bytes 1572872 | tf_op jit(solution)/shard_map/ppermute | solution.py:28
  5.9 50.2 %collective-permute-start.4 = (bf16[1024,256]{1,0:T(8,128)(2,1)S(1)}, bf16[1024,256]{1,0:T(8,128)(2,1)S(1)}, u32[]{:S(2)}, u32[]{:S(2)}) collective-permute-start(bf16[1024,256]{1,0:T(8,128)(2,1)S(1)} %get-tuple-element.25.refs_0_), channel_id=1, source_target_pairs={{0,4},{1,5},{2,6},{3,7},{4,0},{5,1},{6,2},{7,3},{8,12},{9,13},{10,... | collective-permute-start | bytes 1572872 | tf_op jit(solution)/shard_map/ppermute | solution.py:28
  6.4 49.7 %collective-permute-start.3 = (bf16[1024,256]{1,0:T(8,128)(2,1)S(1)}, bf16[1024,256]{1,0:T(8,128)(2,1)S(1)}, u32[]{:S(2)}, u32[]{:S(2)}) collective-permute-start(bf16[1024,256]{1,0:T(8,128)(2,1)S(1)} %get-tuple-element.25.refs_0_), channel_id=1, source_target_pairs={{0,2},{1,3},{2,0},{3,1},{4,6},{5,7},{6,4},{7,5},{8,10},{9,11},{10,... | collective-permute-start | bytes 1572872 | tf_op jit(solution)/shard_map/ppermute | solution.py:28
  6.5 49.6 %collective-permute-start.2 = (bf16[1024,256]{1,0:T(8,128)(2,1)S(1)}, bf16[1024,256]{1,0:T(8,128)(2,1)S(1)}, u32[]{:S(2)}, u32[]{:S(2)}) collective-permute-start(bf16[1024,256]{1,0:T(8,128)(2,1)S(1)} %get-tuple-element.20.refs_0_), channel_id=1, source_target_pairs={{0,6},{1,7},{2,4},{3,5},{4,2},{5,3},{6,0},{7,1},{8,14},{9,15},{10,... | collective-permute-start | bytes 1572872 | tf_op jit(solution)/shard_map/ppermute | solution.py:28
  9.4 46.7 %collective-permute-start.1 = (bf16[1024,256]{1,0:T(8,128)(2,1)S(1)}, bf16[1024,256]{1,0:T(8,128)(2,1)}, u32[]{:S(2)}, u32[]{:S(2)}) collective-permute-start(bf16[1024,256]{1,0:T(8,128)(2,1)S(1)} %get-tuple-element.20.refs_0_), channel_id=1, source_target_pairs={{0,4},{1,5},{2,6},{3,7},{4,0},{5,1},{6,2},{7,3},{8,12},{9,13},{10,... | collective-permute-start | bytes 1572872 | tf_op jit(solution)/shard_map/ppermute | solution.py:28
  18.7 37.4 %collective-permute-start = (bf16[1024,256]{1,0:T(8,128)(2,1)S(1)}, bf16[1024,256]{1,0:T(8,128)(2,1)}, u32[]{:S(2)}, u32[]{:S(2)}) collective-permute-start(bf16[1024,256]{1,0:T(8,128)(2,1)S(1)} %get-tuple-element.20.refs_0_), channel_id=1, source_target_pairs={{0,2},{1,3},{2,0},{3,1},{4,6},{5,7},{6,4},{7,5},{8,10},{9,11},{10,... | collective-permute-start | bytes 1572872 | tf_op jit(solution)/shard_map/ppermute | solution.py:28
  57.2 14.9 %collective-permute-start.10 = (bf16[1024,256]{1,0:T(8,128)(2,1)S(1)}, bf16[1024,256]{1,0:T(8,128)(2,1)S(1)}, u32[]{:S(2)}, u32[]{:S(2)}) collective-permute-start(bf16[1024,256]{1,0:T(8,128)(2,1)S(1)} %get-tuple-element.25.refs_0_), channel_id=1, source_target_pairs={{0,1},{1,0},{2,3},{3,2},{4,5},{5,4},{6,7},{7,6},{8,9},{9,8},{10,11... | collective-permute-start | bytes 1572872 | tf_op jit(solution)/shard_map/ppermute | solution.py:28
  58.2 13.9 %collective-permute-start.11 = (bf16[1024,256]{1,0:T(8,128)(2,1)S(1)}, bf16[1024,256]{1,0:T(8,128)(2,1)S(1)}, u32[]{:S(2)}, u32[]{:S(2)}) collective-permute-start(bf16[1024,256]{1,0:T(8,128)(2,1)S(1)} %collective-permute-done.3.refs_2_), channel_id=1, source_target_pairs={{0,1},{1,0},{2,3},{3,2},{4,5},{5,4},{6,7},{7,6},{8,9},{9,8},{10,11... | collective-permute-start | bytes 1572872 | tf_op jit(solution)/shard_map/ppermute | solution.py:28
  59.0 13.2 %collective-permute-start.12 = (bf16[1024,256]{1,0:T(8,128)(2,1)S(1)}, bf16[1024,256]{1,0:T(8,128)(2,1)S(1)}, u32[]{:S(2)}, u32[]{:S(2)}) collective-permute-start(bf16[1024,256]{1,0:T(8,128)(2,1)S(1)} %collective-permute-done.4.refs_4_), channel_id=1, source_target_pairs={{0,1},{1,0},{2,3},{3,2},{4,5},{5,4},{6,7},{7,6},{8,9},{9,8},{10,11... | collective-permute-start | bytes 1572872 | tf_op jit(solution)/shard_map/ppermute | solution.py:28
  59.7 12.4 %collective-permute-start.13 = (bf16[1024,256]{1,0:T(8,128)(2,1)S(1)}, bf16[1024,256]{1,0:T(8,128)(2,1)S(1)}, u32[]{:S(2)}, u32[]{:S(2)}) collective-permute-start(bf16[1024,256]{1,0:T(8,128)(2,1)S(1)} %collective-permute-done.5.refs_6_), channel_id=1, source_target_pairs={{0,1},{1,0},{2,3},{3,2},{4,5},{5,4},{6,7},{7,6},{8,9},{9,8},{10,11... | collective-permute-start | bytes 1572872 | tf_op jit(solution)/shard_map/ppermute | solution.py:28
  131.1 10.0 %collective-permute-start.25 = (bf16[4096,256]{1,0:T(8,128)(2,1)}, bf16[4096,256]{1,0:T(8,128)(2,1)}, u32[]{:S(2)}, u32[]{:S(2)}) collective-permute-start(bf16[4096,256]{1,0:T(8,128)(2,1)} %constant_dynamic-slice_fusion.4), channel_id=1, source_target_pairs={{0,1},{1,0},{2,3},{3,2},{4,5},{5,4},{6,7},{7,6},{8,9},{9,8},{10,11... | collective-permute-start | bytes 6291464 | tf_op jit(solution)/shard_map/ppermute | solution.py:28
  144.2 14.9 %collective-permute-start.26 = (bf16[1024,256]{1,0:T(8,128)(2,1)S(1)}, bf16[1024,256]{1,0:T(8,128)(2,1)S(1)}, u32[]{:S(2)}, u32[]{:S(2)}) collective-permute-start(bf16[1024,256]{1,0:T(8,128)(2,1)S(1)} %dynamic-slice_convert_fusion.7), channel_id=1, source_target_pairs={{0,2},{1,3},{2,0},{3,1},{4,6},{5,7},{6,4},{7,5},{8,10},{9,11},{10,... | collective-permute-start | bytes 1572872 | tf_op jit(solution)/shard_map/ppermute | solution.py:28
  146.1 14.9 %collective-permute-start.28 = (bf16[1024,256]{1,0:T(8,128)(2,1)S(1)}, bf16[1024,256]{1,0:T(8,128)(2,1)S(1)}, u32[]{:S(2)}, u32[]{:S(2)}) collective-permute-start(bf16[1024,256]{1,0:T(8,128)(2,1)S(1)} %dynamic-slice_convert_fusion.6), channel_id=1, source_target_pairs={{0,4},{1,5},{2,6},{3,7},{4,0},{5,1},{6,2},{7,3},{8,12},{9,13},{10,... | collective-permute-start | bytes 1572872 | tf_op jit(solution)/shard_map/ppermute | solution.py:28
  149.6 20.7 %collective-permute-start.42 = (bf16[1024,256]{1,0:T(8,128)(2,1)S(1)}, bf16[1024,256]{1,0:T(8,128)(2,1)S(1)}, u32[]{:S(2)}, u32[]{:S(2)}) collective-permute-start(bf16[1024,256]{1,0:T(8,128)(2,1)S(1)} %dynamic-slice_convert_fusion.5), channel_id=1, source_target_pairs={{0,2},{1,3},{2,0},{3,1},{4,6},{5,7},{6,4},{7,5},{8,10},{9,11},{10,... | collective-permute-start | bytes 1572872 | tf_op jit(solution)/shard_map/ppermute | solution.py:28
  150.6 21.6 %collective-permute-start.44 = (bf16[1024,256]{1,0:T(8,128)(2,1)S(1)}, bf16[1024,256]{1,0:T(8,128)(2,1)S(1)}, u32[]{:S(2)}, u32[]{:S(2)}) collective-permute-start(bf16[1024,256]{1,0:T(8,128)(2,1)S(1)} %dynamic-slice_convert_fusion.4), channel_id=1, source_target_pairs={{0,4},{1,5},{2,6},{3,7},{4,0},{5,1},{6,2},{7,3},{8,12},{9,13},{10,... | collective-permute-start | bytes 1572872 | tf_op jit(solution)/shard_map/ppermute | solution.py:28
  159.2 18.6 %collective-permute-start.27 = (bf16[512,256]{1,0:T(8,128)(2,1)S(1)}, bf16[512,256]{1,0:T(8,128)(2,1)S(1)}, u32[]{:S(2)}, u32[]{:S(2)}) collective-permute-start(bf16[512,256]{1,0:T(8,128)(2,1)S(1)} %dynamic-slice_convert_fusion.15), channel_id=1, source_target_pairs={{0,4},{1,5},{2,6},{3,7},{4,0},{5,1},{6,2},{7,3},{8,12},{9,13},{10,... | collective-permute-start | bytes 786440 | tf_op jit(solution)/shard_map/ppermute | solution.py:28
  161.2 16.7 %collective-permute-start.29 = (bf16[512,256]{1,0:T(8,128)(2,1)S(1)}, bf16[512,256]{1,0:T(8,128)(2,1)S(1)}, u32[]{:S(2)}, u32[]{:S(2)}) collective-permute-start(bf16[512,256]{1,0:T(8,128)(2,1)S(1)} %dynamic-slice_convert_fusion.14), channel_id=1, source_target_pairs={{0,2},{1,3},{2,0},{3,1},{4,6},{5,7},{6,4},{7,5},{8,10},{9,11},{10,... | collective-permute-start | bytes 786440 | tf_op jit(solution)/shard_map/ppermute | solution.py:28
  170.4 12.1 %collective-permute-start.43 = (bf16[512,256]{1,0:T(8,128)(2,1)S(1)}, bf16[512,256]{1,0:T(8,128)(2,1)S(1)}, u32[]{:S(2)}, u32[]{:S(2)}) collective-permute-start(bf16[512,256]{1,0:T(8,128)(2,1)S(1)} %dynamic-slice_convert_fusion.13), channel_id=1, source_target_pairs={{0,4},{1,5},{2,6},{3,7},{4,0},{5,1},{6,2},{7,3},{8,12},{9,13},{10,... | collective-permute-start | bytes 786440 | tf_op jit(solution)/shard_map/ppermute | solution.py:28
  172.4 22.7 %collective-permute-start.45 = (bf16[512,256]{1,0:T(8,128)(2,1)S(1)}, bf16[512,256]{1,0:T(8,128)(2,1)S(1)}, u32[]{:S(2)}, u32[]{:S(2)}) collective-permute-start(bf16[512,256]{1,0:T(8,128)(2,1)S(1)} %dynamic-slice_convert_fusion.12), channel_id=1, source_target_pairs={{0,2},{1,3},{2,0},{3,1},{4,6},{5,7},{6,4},{7,5},{8,10},{9,11},{10,... | collective-permute-start | bytes 786440 | tf_op jit(solution)/shard_map/ppermute | solution.py:28
  179.1 11.4 %collective-permute-start.31 = (bf16[2,128,256]{2,1,0:T(8,128)(2,1)S(1)}, bf16[2,128,256]{2,1,0:T(8,128)(2,1)S(1)}, u32[]{:S(2)}, u32[]{:S(2)}) collective-permute-start(bf16[2,128,256]{2,1,0:T(8,128)(2,1)S(1)} %get-tuple-element.66), channel_id=1, source_target_pairs={{0,16},{8,24},{16,0},{24,8},{1,17},{9,25},{17,1},{25,9},{2,18},{10... | collective-permute-start | bytes 393224 | tf_op jit(solution)/shard_map/ppermute | solution.py:28
  192.6 13.0 %collective-permute-start.34 = (bf16[2,128,256]{2,1,0:T(8,128)(2,1)S(1)}, bf16[2,128,256]{2,1,0:T(8,128)(2,1)S(1)}, u32[]{:S(2)}, u32[]{:S(2)}) collective-permute-start(bf16[2,128,256]{2,1,0:T(8,128)(2,1)S(1)} %fusion.39), channel_id=1, source_target_pairs={{0,16},{8,24},{16,0},{24,8},{1,17},{9,25},{17,1},{25,9},{2,18},{10... | collective-permute-start | bytes 393224 | tf_op jit(solution)/shard_map/ppermute | solution.py:28
  193.3 12.3 %collective-permute-start.33 = (bf16[2,128,256]{2,1,0:T(8,128)(2,1)S(1)}, bf16[2,128,256]{2,1,0:T(8,128)(2,1)S(1)}, u32[]{:S(2)}, u32[]{:S(2)}) collective-permute-start(bf16[2,128,256]{2,1,0:T(8,128)(2,1)S(1)} %fusion.39), channel_id=1, source_target_pairs={{0,24},{8,16},{16,8},{24,0},{1,25},{9,17},{17,9},{25,1},{2,26},{10... | collective-permute-start | bytes 393224 | tf_op jit(solution)/shard_map/ppermute | solution.py:28
  195.2 12.6 %collective-permute-start.46 = (bf16[2,128,256]{2,1,0:T(8,128)(2,1)S(1)}, bf16[2,128,256]{2,1,0:T(8,128)(2,1)S(1)}, u32[]{:S(2)}, u32[]{:S(2)}) collective-permute-start(bf16[2,128,256]{2,1,0:T(8,128)(2,1)S(1)} %get-tuple-element.58), channel_id=1, source_target_pairs={{0,8},{8,0},{16,24},{24,16},{1,9},{9,1},{17,25},{25,17},{2,10},{10... | collective-permute-start | bytes 393224 | tf_op jit(solution)/shard_map/ppermute | solution.py:28
  196.3 18.8 %collective-permute-start.47 = (bf16[2,128,256]{2,1,0:T(8,128)(2,1)S(1)}, bf16[2,128,256]{2,1,0:T(8,128)(2,1)S(1)}, u32[]{:S(2)}, u32[]{:S(2)}) collective-permute-start(bf16[2,128,256]{2,1,0:T(8,128)(2,1)S(1)} %get-tuple-element.59), channel_id=1, source_target_pairs={{0,16},{8,24},{16,0},{24,8},{1,17},{9,25},{17,1},{25,9},{2,18},{10... | collective-permute-start | bytes 393224 | tf_op jit(solution)/shard_map/ppermute | solution.py:28
  199.7 15.3 %collective-permute-start.48 = (bf16[2,128,256]{2,1,0:T(8,128)(2,1)S(1)}, bf16[2,128,256]{2,1,0:T(8,128)(2,1)S(1)}, u32[]{:S(2)}, u32[]{:S(2)}) collective-permute-start(bf16[2,128,256]{2,1,0:T(8,128)(2,1)S(1)} %get-tuple-element.60), channel_id=1, source_target_pairs={{0,24},{8,16},{16,8},{24,0},{1,25},{9,17},{17,9},{25,1},{2,26},{10... | collective-permute-start | bytes 393224 | tf_op jit(solution)/shard_map/ppermute | solution.py:28
  205.7 14.1 %collective-permute-start.36 = (bf16[512,256]{1,0:T(8,128)(2,1)S(1)}, bf16[512,256]{1,0:T(8,128)(2,1)S(1)}, u32[]{:S(2)}, u32[]{:S(2)}) collective-permute-start(bf16[512,256]{1,0:T(8,128)(2,1)S(1)} %get-tuple-element.90), channel_id=1, source_target_pairs={{0,4},{1,5},{2,6},{3,7},{4,0},{5,1},{6,2},{7,3},{8,12},{9,13},{10,... | collective-permute-start | bytes 786440 | tf_op jit(solution)/shard_map/ppermute | solution.py:28
  206.8 13.1 %collective-permute-start.38 = (bf16[512,256]{1,0:T(8,128)(2,1)S(1)}, bf16[512,256]{1,0:T(8,128)(2,1)S(1)}, u32[]{:S(2)}, u32[]{:S(2)}) collective-permute-start(bf16[512,256]{1,0:T(8,128)(2,1)S(1)} %get-tuple-element.91), channel_id=1, source_target_pairs={{0,2},{1,3},{2,0},{3,1},{4,6},{5,7},{6,4},{7,5},{8,10},{9,11},{10,... | collective-permute-start | bytes 786440 | tf_op jit(solution)/shard_map/ppermute | solution.py:28
  217.4 11.7 %collective-permute-start.50 = (bf16[2,128,256]{2,1,0:T(8,128)(2,1)S(1)}, bf16[2,128,256]{2,1,0:T(8,128)(2,1)S(1)}, u32[]{:S(2)}, u32[]{:S(2)}) collective-permute-start(bf16[2,128,256]{2,1,0:T(8,128)(2,1)S(1)} %fusion.29), channel_id=1, source_target_pairs={{0,16},{8,24},{16,0},{24,8},{1,17},{9,25},{17,1},{25,9},{2,18},{10... | collective-permute-start | bytes 393224 | tf_op jit(solution)/shard_map/ppermute | solution.py:28
  217.9 11.1 %collective-permute-start.49 = (bf16[2,128,256]{2,1,0:T(8,128)(2,1)S(1)}, bf16[2,128,256]{2,1,0:T(8,128)(2,1)S(1)}, u32[]{:S(2)}, u32[]{:S(2)}) collective-permute-start(bf16[2,128,256]{2,1,0:T(8,128)(2,1)S(1)} %fusion.29), channel_id=1, source_target_pairs={{0,24},{8,16},{16,8},{24,0},{1,25},{9,17},{17,9},{25,1},{2,26},{10... | collective-permute-start | bytes 393224 | tf_op jit(solution)/shard_map/ppermute | solution.py:28
  220.0 12.8 %collective-permute-start.39 = (bf16[1024,256]{1,0:T(8,128)(2,1)S(1)}, bf16[1024,256]{1,0:T(8,128)(2,1)S(1)}, u32[]{:S(2)}, u32[]{:S(2)}) collective-permute-start(bf16[1024,256]{1,0:T(8,128)(2,1)S(1)} %pad_maximum_fusion.6), channel_id=1, source_target_pairs={{0,4},{1,5},{2,6},{3,7},{4,0},{5,1},{6,2},{7,3},{8,12},{9,13},{10,... | collective-permute-start | bytes 1572872 | tf_op jit(solution)/shard_map/ppermute | solution.py:28
  229.1 14.9 %collective-permute-start.37 = (bf16[1024,256]{1,0:T(8,128)(2,1)S(1)}, bf16[1024,256]{1,0:T(8,128)(2,1)S(1)}, u32[]{:S(2)}, u32[]{:S(2)}) collective-permute-start(bf16[1024,256]{1,0:T(8,128)(2,1)S(1)} %pad_maximum_fusion.5), channel_id=1, source_target_pairs={{0,2},{1,3},{2,0},{3,1},{4,6},{5,7},{6,4},{7,5},{8,10},{9,11},{10,... | collective-permute-start | bytes 1572872 | tf_op jit(solution)/shard_map/ppermute | solution.py:28
  230.7 13.7 %collective-permute-start.52 = (bf16[512,256]{1,0:T(8,128)(2,1)S(1)}, bf16[512,256]{1,0:T(8,128)(2,1)S(1)}, u32[]{:S(2)}, u32[]{:S(2)}) collective-permute-start(bf16[512,256]{1,0:T(8,128)(2,1)S(1)} %get-tuple-element.82), channel_id=1, source_target_pairs={{0,4},{1,5},{2,6},{3,7},{4,0},{5,1},{6,2},{7,3},{8,12},{9,13},{10,... | collective-permute-start | bytes 786440 | tf_op jit(solution)/shard_map/ppermute | solution.py:28
  231.3 15.6 %collective-permute-start.54 = (bf16[512,256]{1,0:T(8,128)(2,1)S(1)}, bf16[512,256]{1,0:T(8,128)(2,1)S(1)}, u32[]{:S(2)}, u32[]{:S(2)}) collective-permute-start(bf16[512,256]{1,0:T(8,128)(2,1)S(1)} %get-tuple-element.83), channel_id=1, source_target_pairs={{0,2},{1,3},{2,0},{3,1},{4,6},{5,7},{6,4},{7,5},{8,10},{9,11},{10,... | collective-permute-start | bytes 786440 | tf_op jit(solution)/shard_map/ppermute | solution.py:28
  244.3 15.2 %collective-permute-start.40 = (bf16[4096,256]{1,0:T(8,128)(2,1)S(1)}, bf16[4096,256]{1,0:T(8,128)(2,1)S(1)}, u32[]{:S(2)}, u32[]{:S(2)}) collective-permute-start(bf16[4096,256]{1,0:T(8,128)(2,1)S(1)} %pad_maximum_fusion), channel_id=1, source_target_pairs={{0,1},{1,0},{2,3},{3,2},{4,5},{5,4},{6,7},{7,6},{8,9},{9,8},{10,11... | collective-permute-start | bytes 6291464 | tf_op jit(solution)/shard_map/ppermute | solution.py:28
  247.1 11.9 %collective-permute-start.55 = (bf16[1024,256]{1,0:T(8,128)(2,1)S(1)}, bf16[1024,256]{1,0:T(8,128)(2,1)S(1)}, u32[]{:S(2)}, u32[]{:S(2)}) collective-permute-start(bf16[1024,256]{1,0:T(8,128)(2,1)S(1)} %pad_maximum_fusion.9), channel_id=1, source_target_pairs={{0,4},{1,5},{2,6},{3,7},{4,0},{5,1},{6,2},{7,3},{8,12},{9,13},{10,... | collective-permute-start | bytes 1572872 | tf_op jit(solution)/shard_map/ppermute | solution.py:28
  247.2 11.9 %collective-permute-start.53 = (bf16[1024,256]{1,0:T(8,128)(2,1)S(1)}, bf16[1024,256]{1,0:T(8,128)(2,1)S(1)}, u32[]{:S(2)}, u32[]{:S(2)}) collective-permute-start(bf16[1024,256]{1,0:T(8,128)(2,1)S(1)} %pad_maximum_fusion.8), channel_id=1, source_target_pairs={{0,2},{1,3},{2,0},{3,1},{4,6},{5,7},{6,4},{7,5},{8,10},{9,11},{10,... | collective-permute-start | bytes 1572872 | tf_op jit(solution)/shard_map/ppermute | solution.py:28
  259.5 10.3 %collective-permute-start.56 = (bf16[4096,256]{1,0:T(8,128)(2,1)S(1)}, bf16[4096,256]{1,0:T(8,128)(2,1)S(1)}, u32[]{:S(2)}, u32[]{:S(2)}) collective-permute-start(bf16[4096,256]{1,0:T(8,128)(2,1)S(1)} %pad_maximum_fusion.1), channel_id=1, source_target_pairs={{0,1},{1,0},{2,3},{3,2},{4,5},{5,4},{6,7},{7,6},{8,9},{9,8},{10,11... | collective-permute-start | bytes 6291464 | tf_op jit(solution)/shard_map/ppermute | solution.py:28
  349.9 14.9 %collective-permute-start.70 = (bf16[2,1,512,256]{3,2,1,0:T(8,128)(2,1)S(1)}, bf16[2,1,512,256]{3,2,1,0:T(8,128)(2,1)S(1)}, u32[]{:S(2)}, u32[]{:S(2)}) collective-permute-start(bf16[2,1,512,256]{3,2,1,0:T(8,128)(2,1)S(1)} %dynamic-slice_convert_fusion.3), channel_id=1, source_target_pairs={{0,2},{1,3},{2,0},{3,1},{4,6},{5,7},{6,4},{7,5},{8,10},{9,11},{10,... | collective-permute-start | bytes 1572872 | tf_op jit(solution)/shard_map/ppermute | solution.py:28
  350.7 15.8 %collective-permute-start.72 = (bf16[1,2,512,256]{3,2,1,0:T(8,128)(2,1)S(1)}, bf16[1,2,512,256]{3,2,1,0:T(8,128)(2,1)S(1)}, u32[]{:S(2)}, u32[]{:S(2)}) collective-permute-start(bf16[1,2,512,256]{3,2,1,0:T(8,128)(2,1)S(1)} %dynamic-slice_convert_fusion.2), channel_id=1, source_target_pairs={{0,4},{1,5},{2,6},{3,7},{4,0},{5,1},{6,2},{7,3},{8,12},{9,13},{10,... | collective-permute-start | bytes 1572872 | tf_op jit(solution)/shard_map/ppermute | solution.py:28
  357.5 18.5 %collective-permute-start.77 = (bf16[2,1,512,256]{3,2,1,0:T(8,128)(2,1)S(1)}, bf16[2,1,512,256]{3,2,1,0:T(8,128)(2,1)S(1)}, u32[]{:S(2)}, u32[]{:S(2)}) collective-permute-start(bf16[2,1,512,256]{3,2,1,0:T(8,128)(2,1)S(1)} %dynamic-slice_convert_fusion.1), channel_id=1, source_target_pairs={{0,2},{1,3},{2,0},{3,1},{4,6},{5,7},{6,4},{7,5},{8,10},{9,11},{10,... | collective-permute-start | bytes 1572872 | tf_op jit(solution)/shard_map/ppermute | solution.py:28
  359.0 18.7 %collective-permute-start.79 = (bf16[1,2,512,256]{3,2,1,0:T(8,128)(2,1)S(1)}, bf16[1,2,512,256]{3,2,1,0:T(8,128)(2,1)S(1)}, u32[]{:S(2)}, u32[]{:S(2)}) collective-permute-start(bf16[1,2,512,256]{3,2,1,0:T(8,128)(2,1)S(1)} %dynamic-slice_convert_fusion), channel_id=1, source_target_pairs={{0,4},{1,5},{2,6},{3,7},{4,0},{5,1},{6,2},{7,3},{8,12},{9,13},{10,... | collective-permute-start | bytes 1572872 | tf_op jit(solution)/shard_map/ppermute | solution.py:28
  364.9 17.5 %collective-permute-start.71 = (bf16[1,512,256]{2,1,0:T(8,128)(2,1)S(1)}, bf16[1,512,256]{2,1,0:T(8,128)(2,1)S(1)}, u32[]{:S(2)}, u32[]{:S(2)}) collective-permute-start(bf16[1,512,256]{2,1,0:T(8,128)(2,1)S(1)} %fusion.14), channel_id=1, source_target_pairs={{0,4},{1,5},{2,6},{3,7},{4,0},{5,1},{6,2},{7,3},{8,12},{9,13},{10,... | collective-permute-start | bytes 786440 | tf_op jit(solution)/shard_map/ppermute | solution.py:28
  366.6 15.9 %collective-permute-start.73 = (bf16[1,512,256]{2,1,0:T(8,128)(2,1)S(1)}, bf16[1,512,256]{2,1,0:T(8,128)(2,1)S(1)}, u32[]{:S(2)}, u32[]{:S(2)}) collective-permute-start(bf16[1,512,256]{2,1,0:T(8,128)(2,1)S(1)} %fusion.15), channel_id=1, source_target_pairs={{0,2},{1,3},{2,0},{3,1},{4,6},{5,7},{6,4},{7,5},{8,10},{9,11},{10,... | collective-permute-start | bytes 786440 | tf_op jit(solution)/shard_map/ppermute | solution.py:28
  376.1 10.7 %collective-permute-start.78 = (bf16[1,512,256]{2,1,0:T(8,128)(2,1)S(1)}, bf16[1,512,256]{2,1,0:T(8,128)(2,1)S(1)}, u32[]{:S(2)}, u32[]{:S(2)}) collective-permute-start(bf16[1,512,256]{2,1,0:T(8,128)(2,1)S(1)} %fusion.16), channel_id=1, source_target_pairs={{0,4},{1,5},{2,6},{3,7},{4,0},{5,1},{6,2},{7,3},{8,12},{9,13},{10,... | collective-permute-start | bytes 786440 | tf_op jit(solution)/shard_map/ppermute | solution.py:28
  384.7 18.4 %collective-permute-start.75 = (bf16[64,1024]{1,0:T(8,128)(2,1)S(1)}, bf16[64,1024]{1,0:T(8,128)(2,1)S(1)}, u32[]{:S(2)}, u32[]{:S(2)}) collective-permute-start(bf16[64,1024]{1,0:T(8,128)(2,1)S(1)} %get-tuple-element.50), channel_id=1, source_target_pairs={{0,16},{8,24},{16,0},{24,8},{1,17},{9,25},{17,1},{25,9},{2,18},{10... | collective-permute-start | bytes 393224 | tf_op jit(solution)/shard_map/ppermute | solution.py:28
  387.4 15.7 %collective-permute-start.81 = (bf16[64,1024]{1,0:T(8,128)(2,1)S(1)}, bf16[64,1024]{1,0:T(8,128)(2,1)S(1)}, u32[]{:S(2)}, u32[]{:S(2)}) collective-permute-start(bf16[64,1024]{1,0:T(8,128)(2,1)S(1)} %get-tuple-element.51), channel_id=1, source_target_pairs={{0,8},{8,0},{16,24},{24,16},{1,9},{9,1},{17,25},{25,17},{2,10},{10... | collective-permute-start | bytes 393224 | tf_op jit(solution)/shard_map/ppermute | solution.py:28
  388.0 15.1 %collective-permute-start.83 = (bf16[64,1024]{1,0:T(8,128)(2,1)S(1)}, bf16[64,1024]{1,0:T(8,128)(2,1)S(1)}, u32[]{:S(2)}, u32[]{:S(2)}) collective-permute-start(bf16[64,1024]{1,0:T(8,128)(2,1)S(1)} %get-tuple-element.52), channel_id=1, source_target_pairs={{0,24},{8,16},{16,8},{24,0},{1,25},{9,17},{17,9},{25,1},{2,26},{10... | collective-permute-start | bytes 393224 | tf_op jit(solution)/shard_map/ppermute | solution.py:28
  389.7 17.4 %collective-permute-start.82 = (bf16[64,1024]{1,0:T(8,128)(2,1)S(1)}, bf16[64,1024]{1,0:T(8,128)(2,1)S(1)}, u32[]{:S(2)}, u32[]{:S(2)}) collective-permute-start(bf16[64,1024]{1,0:T(8,128)(2,1)S(1)} %get-tuple-element.53), channel_id=1, source_target_pairs={{0,16},{8,24},{16,0},{24,8},{1,17},{9,25},{17,1},{25,9},{2,18},{10... | collective-permute-start | bytes 393224 | tf_op jit(solution)/shard_map/ppermute | solution.py:28
  (56 other events, 397.8 us)
where the time goes:
time: 414 us; the launch traced here: 408 us
  waiting for transfers between devices  149 us (36%)
  starting transfers between devices  90.2 us (22%)
  matrix products  70 us (17%)
  Pallas kernels  63.6 us (15%)
  local copies, waits for them, and re-layouts  17.1 us (4%)
  other arithmetic  15.7 us (4%)
    ppermute x84, waiting for transfers between devices, swap(): return lax.ppermute(value, axis, pairs)  149 us
    ppermute x84, starting transfers between devices, swap(): return lax.ppermute(value, axis, pairs)  90.2 us
    pallas_call x1, Pallas kernels, differences(): pl.pallas_call(difference_kernel, out_shape=(jax.ShapeDtypeStruct((rows,...  35.4 us
    dot_general x4, matrix products, backward(): lax.dot_general(delta, basis, (((0,), (0,)), ((), ())), preferred_element...  31.7 us
    dot_general x4, matrix products, forward(): return jnp.dot(delta, right, preferred_element_type=jnp.float32)  27 us
    pallas_call x2, Pallas kernels, inverse_factor(): pl.pallas_call(inverse_factor_kernel, out_shape=jax.ShapeDtypeStruct(gram...  24.7 us
    unnamed x43, local copies, waits for them, and re-layouts  11.9 us
    dot_general x8, matrix products, product(): lax.dot_general(left, right, dims, precision=HIGHEST, preferred_element_t...  11.3 us
  transfers between devices with their start and end apart: 84, of which 47 were waited for; matrix products, arithmetic and copies ran while one was open for 12% of the time, Pallas kernels for 9%

commit v1 on v0

--- a/solution.py
+++ b/solution.py
@@ -300,8 +300,10 @@
     bits = chip_bits()
     totals = [reduce_half(backward(delta, basis), "col", 1, 0) for delta, basis in zip(deltas, bases)]
     columns = []
-    for shares in reduce_chips([two_shares(total, 0) for total in totals], False):
-        value = gather_rows(reduce_rows(jnp.stack(shares), 1).astype(jnp.bfloat16), 1)
+    shares_of = reduce_chips([two_shares(total, 0) for total in totals], False)
+    for shares in shares_of:
+        value = reduce_rows(jnp.stack(shares), 1)
+        value = gather_rows(value.astype(jnp.bfloat16), 1)
         shares = []
         for index, order in ((0, bits[::-1]), (1, bits)):
             share = value[index]
@@ -333,18 +335,27 @@
     totals = [core_sum(delta, basis.astype(jnp.bfloat16)) for delta, basis in zip(deltas, bases)]
     bases, totals[-1] = lax.optimization_barrier((bases, totals[-1]))
     shares_of = reduce_chips([two_shares(total, total.ndim - 2) for total in totals], True)
-    return [reduce_rows(transposed(shares), 0) for shares in shares_of], bases
+    downs = []
+    for shares in shares_of:
+        downs.append(reduce_rows(transposed(shares), 0))
+    return downs, bases
 
 
 def extract(base_flat, adjusted_flat, omega):
     matrices, _, _ = omega.shape
     hidden_units = base_flat.shape[1] * lax.axis_size("row") * lax.axis_size("col")
     every = range(matrices)
-    near = [near_parts(omega[m]) for m in every]
+    near = []
+    for m in every:
+        near.append(near_parts(omega[m]))
     deltas = differences(adjusted_flat, base_flat)
-    deltas, near = lax.optimization_barrier((deltas, near))
+    deltas, near[0] = lax.optimization_barrier((deltas, near[0]))
     place = lax.axis_index("col")
-    panels = [forward(deltas[m], assemble(with_other_core(near[m]), place)) for m in every]
+    panels = []
+    for m in every:
+        parts = with_other_core(near[m])
+        right = assemble(parts, place)
+        panels.append(forward(deltas[m], right))
     inverses = factors(panels)
     first = [product(panels[m], inverses[m], (1, 1)).astype(jnp.bfloat16) for m in every]
     columns = all_columns(deltas, first)

time: 414 us -> 443 us (1.070)
  waiting for transfers between devices: 149 us -> 178 us
    ppermute x84, waiting for transfers between devices: 149 us -> 178 us  [swap(): return lax.ppermute(value, axis, pairs)]
  transfers between devices with their start and end apart: 84 -> 84, of which waited for: 47 -> 46; matrix products, arithmetic and copies ran while one was open for 12% -> 12% of each run, Pallas kernels for 9% -> 9%
where the time goes in v1:
time: 443 us; the launch traced here: 437 us
  waiting for transfers between devices  178 us (40%)
  starting transfers between devices  90.6 us (20%)
  matrix products  70 us (16%)
  Pallas kernels  63.6 us (14%)
  local copies, waits for them, and re-layouts  16.9 us (4%)
  other arithmetic  15.7 us (4%)
    ppermute x84, waiting for transfers between devices, swap(): return lax.ppermute(value, axis, pairs)  178 us
    ppermute x84, starting transfers between devices, swap(): return lax.ppermute(value, axis, pairs)  90.6 us
    pallas_call x1, Pallas kernels, differences(): pl.pallas_call(difference_kernel, out_shape=(jax.ShapeDtypeStruct((rows,...  35.4 us
    dot_general x4, matrix products, backward(): lax.dot_general(delta, basis, (((0,), (0,)), ((), ())), preferred_element...  31.7 us
    dot_general x4, matrix products, forward(): return jnp.dot(delta, right, preferred_element_type=jnp.float32)  27 us
    pallas_call x2, Pallas kernels, inverse_factor(): pl.pallas_call(inverse_factor_kernel, out_shape=jax.ShapeDtypeStruct(gram...  24.8 us
    unnamed x43, local copies, waits for them, and re-layouts  11.9 us
    dot_general x8, matrix products, product(): lax.dot_general(left, right, dims, precision=HIGHEST, preferred_element_t...  11.4 us
  transfers between devices with their start and end apart: 84, of which 46 were waited for; matrix products, arithmetic and copies ran while one was open for 12% of the time, Pallas kernels for 9%

profile of v1, /device:TPU:0, one launch (start us, length us, event | category | flops | bytes accessed | tf_op | source)
XLA Modules:
  0.0 437.0 jit_solution(12577972347346989660)
XLA Ops:
  1.9 4.0 collective-permute-start.2
  9.9 8.9 %collective-permute-done.2.refs_6_ = bf16[1024,256]{1,0:T(8,128)(2,1)S(1)} collective-permute-done((bf16[1024,256]{1,0:T(8,128)(2,1)S(1)}, bf16[1024,256]{1,0:T(8,128)(2,1)S(1)}, u32[]{:S(2)}, u32[]{:S(2)}) %collective-permute-start.2) | collective-permute-done | bytes 524320 | tf_op jit(solution)/shard_map/ppermute | solution.py:28
  20.7 19.7 %collective-permute-done.1.refs_4_ = bf16[1024,256]{1,0:T(8,128)(2,1)S(1)} collective-permute-done((bf16[1024,256]{1,0:T(8,128)(2,1)S(1)}, bf16[1024,256]{1,0:T(8,128)(2,1)S(1)}, u32[]{:S(2)}, u32[]{:S(2)}) %collective-permute-start.1) | collective-permute-done | bytes 524320 | tf_op jit(solution)/shard_map/ppermute | solution.py:28
  40.9 10.7 %collective-permute-done.10.refs_4_ = bf16[1024,256]{1,0:T(8,128)(2,1)} collective-permute-done((bf16[1024,256]{1,0:T(8,128)(2,1)S(1)}, bf16[1024,256]{1,0:T(8,128)(2,1)}, u32[]{:S(2)}, u32[]{:S(2)}) %collective-permute-start.10) | collective-permute-done | bytes 524320 | tf_op jit(solution)/shard_map/ppermute | solution.py:28
  52.1 35.4 %difference.1 = (bf16[924,8192]{1,0:T(8,128)(2,1)}, bf16[924,8192]{1,0:T(8,128)(2,1)}) custom-call(bf16[924,2,8192]{2,1,0:T(2,128)(2,1)} %bitcast.139, bf16[924,2,8192]{2,1,0:T(2,128)(2,1)} %bitcast.140), custom_call_target="tpu_custom_call" | custom-call | tf_op jit(solution)/shard_map/difference/pallas_call | solution.py:208
  90.6 7.8 %fusion.53 = f32[924,256]{1,0:T(8,128)S(1)} fusion(bf16[924,8192]{1,0:T(8,128)(2,1)} %get-tuple-element.20, bf16[8192,256]{1,0:T(8,128)(2,1)S(1)} %assemble.3), kind=kOutput, calls=%fused_computation.227 | convolution fusion | flops 3875536896 | bytes 20279296 | tf_op jit(solution)/shard_map/dot_general | solution.py:246
  101.2 4.1 fusion.52
  113.2 2.7 collective-permute-done.17
  116.9 3.7 collective-permute-start.20
  121.4 2.2 collective-permute-done.20
  123.5 2.6 collective-permute-done.19
  131.1 2.4 collective-permute-done.21
  135.2 12.5 %inverse_factor.2 = f32[2,256,256]{2,1,0:T(8,128)S(1)} custom-call(f32[2,256,256]{2,1,0:T(8,128)S(1)} %pad_maximum_fusion.3.gram_ref), custom_call_target="tpu_custom_call" | custom-call | tf_op jit(solution)/shard_map/inverse_factor/pallas_call | solution.py:156
  148.6 10.3 %convolution_convert_fusion.3 = bf16[8192,256]{1,0:T(8,128)(2,1)S(1)} fusion(bf16[924,8192]{1,0:T(8,128)(2,1)} %get-tuple-element.15, bf16[924,256]{1,0:T(8,128)(2,1)S(1)} %convolution_convert_fusion.5), kind=kOutput, calls=%fused_computation.3 | convolution fusion | flops 3877634048 | bytes 19806208 | tf_op jit(solution)/shard_map/dot_general | solution.py:250
  162.6 5.6 %convolution_convert_fusion.2 = bf16[8192,256]{1,0:T(8,128)(2,1)S(1)} fusion(bf16[924,8192]{1,0:T(8,128)(2,1)S(1)} %bitcast.146, bf16[924,256]{1,0:T(8,128)(2,1)S(1)} %convolution_convert_fusion.4), kind=kOutput, calls=%fused_computation.2 | convolution fusion | flops 3877634048 | bytes 19806208 | tf_op jit(solution)/shard_map/dot_general | solution.py:250
  170.5 2.7 convert_add_fusion.1
  175.7 2.0 convert_add_fusion
  180.3 8.1 %collective-permute-done.26 = bf16[1024,256]{1,0:T(8,128)(2,1)S(1)} collective-permute-done((bf16[1024,256]{1,0:T(8,128)(2,1)S(1)}, bf16[1024,256]{1,0:T(8,128)(2,1)S(1)}, u32[]{:S(2)}, u32[]{:S(2)}) %collective-permute-start.26) | collective-permute-done | bytes 524320 | tf_op jit(solution)/shard_map/ppermute | solution.py:28
  190.8 8.8 %collective-permute-done.42 = bf16[1024,256]{1,0:T(8,128)(2,1)S(1)} collective-permute-done((bf16[1024,256]{1,0:T(8,128)(2,1)S(1)}, bf16[1024,256]{1,0:T(8,128)(2,1)S(1)}, u32[]{:S(2)}, u32[]{:S(2)}) %collective-permute-start.42) | collective-permute-done | bytes 524320 | tf_op jit(solution)/shard_map/ppermute | solution.py:28
  202.1 3.8 collective-permute-done.27
  207.2 2.2 collective-permute-start.31
  211.4 7.2 %collective-permute-done.31 = bf16[2,128,256]{2,1,0:T(8,128)(2,1)S(1)} collective-permute-done((bf16[2,128,256]{2,1,0:T(8,128)(2,1)S(1)}, bf16[2,128,256]{2,1,0:T(8,128)(2,1)S(1)}, u32[]{:S(2)}, u32[]{:S(2)}) %collective-permute-start.31) | collective-permute-done | bytes 131104 | tf_op jit(solution)/shard_map/ppermute | solution.py:28
  218.7 2.0 collective-permute-start.35
  229.6 4.1 collective-permute-done.34
  235.9 7.3 %collective-permute-done.47 = bf16[2,128,256]{2,1,0:T(8,128)(2,1)S(1)} collective-permute-done((bf16[2,128,256]{2,1,0:T(8,128)(2,1)S(1)}, bf16[2,128,256]{2,1,0:T(8,128)(2,1)S(1)}, u32[]{:S(2)}, u32[]{:S(2)}) %collective-permute-start.47) | collective-permute-done | bytes 131104 | tf_op jit(solution)/shard_map/ppermute | solution.py:28
  243.3 2.2 collective-permute-start.51
  249.6 7.6 %collective-permute-done.50 = bf16[2,128,256]{2,1,0:T(8,128)(2,1)S(1)} collective-permute-done((bf16[2,128,256]{2,1,0:T(8,128)(2,1)S(1)}, bf16[2,128,256]{2,1,0:T(8,128)(2,1)S(1)}, u32[]{:S(2)}, u32[]{:S(2)}) %collective-permute-start.50) | collective-permute-done | bytes 131104 | tf_op jit(solution)/shard_map/ppermute | solution.py:28
  262.9 7.0 %collective-permute-done.37 = bf16[1024,256]{1,0:T(8,128)(2,1)S(1)} collective-permute-done((bf16[1024,256]{1,0:T(8,128)(2,1)S(1)}, bf16[1024,256]{1,0:T(8,128)(2,1)S(1)}, u32[]{:S(2)}, u32[]{:S(2)}) %collective-permute-start.37) | collective-permute-done | bytes 524320 | tf_op jit(solution)/shard_map/ppermute | solution.py:28
  270.3 2.4 collective-permute-done.54
  272.8 3.8 collective-permute-start.55
  277.0 9.8 %collective-permute-done.55 = bf16[1024,256]{1,0:T(8,128)(2,1)S(1)} collective-permute-done((bf16[1024,256]{1,0:T(8,128)(2,1)S(1)}, bf16[1024,256]{1,0:T(8,128)(2,1)S(1)}, u32[]{:S(2)}, u32[]{:S(2)}) %collective-permute-start.55) | collective-permute-done | bytes 524320 | tf_op jit(solution)/shard_map/ppermute | solution.py:28
  289.6 7.5 %fusion = f32[924,256]{1,0:T(8,128)S(1)} fusion(bf16[924,8192]{1,0:T(8,128)(2,1)} %get-tuple-element.15, bf16[4096,256]{1,0:T(8,128)(2,1)S(1)} %get-tuple-element.37, bf16[4096,256]{1,0:T(8,128)(2,1)S(1)} %get-tuple-element.36), kind=kOutput, calls=%fused_computation.4 | convolution fusion | flops 3883925504 | bytes 20279296 | tf_op jit(solution)/shard_map/dot_general | solution.py:246
  299.8 7.6 %fusion.4 = f32[924,256]{1,0:T(8,128)S(1)} fusion(bf16[924,8192]{1,0:T(8,128)(2,1)} %get-tuple-element.20, bf16[4096,256]{1,0:T(8,128)(2,1)S(1)} %get-tuple-element.33, bf16[4096,256]{1,0:T(8,128)(2,1)S(1)} %get-tuple-element.32), kind=kOutput, calls=%fused_computation.8 | convolution fusion | flops 3883925504 | bytes 20279296 | tf_op jit(solution)/shard_map/dot_general | solution.py:246
  318.1 5.1 %collective-permute-start.62 = (f32[2,32,256]{2,1,0:T(8,128)S(1)}, f32[2,32,256]{2,1,0:T(8,128)S(1)}, u32[]{:S(2)}, u32[]{:S(2)}) collective-permute-start(f32[2,32,256]{2,1,0:T(8,128)S(1)} %add_add_fusion.1), channel_id=1, source_target_pairs={{0,16},{8,24},{16,0},{24,8},{1,17},{9,25},{17,1},{25,9},{2,18},{10... | collective-permute-start | bytes 196616 | tf_op jit(solution)/shard_map/ppermute | solution.py:28
  324.2 4.2 collective-permute-done.62
  337.5 12.3 %inverse_factor.3 = f32[2,256,256]{2,1,0:T(8,128)S(1)} custom-call(f32[2,256,256]{2,1,0:T(8,128)S(1)} %pad_maximum_fusion.10.gram_ref), custom_call_target="tpu_custom_call" | custom-call | tf_op jit(solution)/shard_map/inverse_factor/pallas_call | solution.py:156
  352.0 10.2 %convolution_convert_fusion = bf16[8192,256]{1,0:T(8,128)(2,1)S(1)} fusion(bf16[924,8192]{1,0:T(8,128)(2,1)} %get-tuple-element.15, f32[924,256]{1,0:T(8,128)S(1)} %fusion.45), kind=kOutput, calls=%fused_computation | convolution fusion | flops 3877870592 | bytes 20279296 | tf_op jit(solution)/shard_map/dot_general | solution.py:250
  365.1 5.5 %convolution_convert_fusion.1 = bf16[8192,256]{1,0:T(8,128)(2,1)S(1)} fusion(bf16[924,8192]{1,0:T(8,128)(2,1)S(1)} %bitcast.148, f32[924,256]{1,0:T(8,128)S(1)} %fusion.44), kind=kOutput, calls=%fused_computation.1 | convolution fusion | flops 3877870592 | bytes 20279296 | tf_op jit(solution)/shard_map/dot_general | solution.py:250
  370.6 2.0 copy-done.5
  374.5 2.7 add_bitcast_fusion
  379.8 2.0 add_bitcast_fusion.1
  382.5 2.7 copy.10
  387.4 5.1 %collective-permute-done.70 = bf16[2,1,512,256]{3,2,1,0:T(8,128)(2,1)S(1)} collective-permute-done((bf16[2,1,512,256]{3,2,1,0:T(8,128)(2,1)S(1)}, bf16[2,1,512,256]{3,2,1,0:T(8,128)(2,1)S(1)}, u32[]{:S(2)}, u32[]{:S(2)}) %collective-permute-start.70) | collective-permute-done | bytes 524320 | tf_op jit(solution)/shard_map/ppermute | solution.py:28
  394.9 8.8 %collective-permute-done.77 = bf16[2,1,512,256]{3,2,1,0:T(8,128)(2,1)S(1)} collective-permute-done((bf16[2,1,512,256]{3,2,1,0:T(8,128)(2,1)S(1)}, bf16[2,1,512,256]{3,2,1,0:T(8,128)(2,1)S(1)}, u32[]{:S(2)}, u32[]{:S(2)}) %collective-permute-start.77) | collective-permute-done | bytes 524320 | tf_op jit(solution)/shard_map/ppermute | solution.py:28
  406.1 5.0 %collective-permute-done.71 = bf16[1,512,256]{2,1,0:T(8,128)(2,1)S(1)} collective-permute-done((bf16[1,512,256]{2,1,0:T(8,128)(2,1)S(1)}, bf16[1,512,256]{2,1,0:T(8,128)(2,1)S(1)}, u32[]{:S(2)}, u32[]{:S(2)}) %collective-permute-start.71) | collective-permute-done | bytes 262176 | tf_op jit(solution)/shard_map/ppermute | solution.py:28
  413.1 2.1 collective-permute-start.75
  420.3 11.7 %collective-permute-done.75 = bf16[64,1024]{1,0:T(8,128)(2,1)S(1)} collective-permute-done((bf16[64,1024]{1,0:T(8,128)(2,1)S(1)}, bf16[64,1024]{1,0:T(8,128)(2,1)S(1)}, u32[]{:S(2)}, u32[]{:S(2)}) %collective-permute-start.75) | collective-permute-done | bytes 131104 | tf_op jit(solution)/shard_map/ppermute | solution.py:28
  432.0 3.8 collective-permute-done.82
  (281 shorter events, 123.3 us)
Async XLA Ops:
  1.9 16.9 %collective-permute-start.2 = (bf16[1024,256]{1,0:T(8,128)(2,1)S(1)}, bf16[1024,256]{1,0:T(8,128)(2,1)S(1)}, u32[]{:S(2)}, u32[]{:S(2)}) collective-permute-start(bf16[1024,256]{1,0:T(8,128)(2,1)S(1)} %get-tuple-element.16.refs_0_), channel_id=1, source_target_pairs={{0,6},{1,7},{2,4},{3,5},{4,2},{5,3},{6,0},{7,1},{8,14},{9,15},{10,... | collective-permute-start | bytes 1572872 | tf_op jit(solution)/shard_map/ppermute | solution.py:28
  5.9 34.5 %collective-permute-start.1 = (bf16[1024,256]{1,0:T(8,128)(2,1)S(1)}, bf16[1024,256]{1,0:T(8,128)(2,1)S(1)}, u32[]{:S(2)}, u32[]{:S(2)}) collective-permute-start(bf16[1024,256]{1,0:T(8,128)(2,1)S(1)} %get-tuple-element.16.refs_0_), channel_id=1, source_target_pairs={{0,4},{1,5},{2,6},{3,7},{4,0},{5,1},{6,2},{7,3},{8,12},{9,13},{10,... | collective-permute-start | bytes 1572872 | tf_op jit(solution)/shard_map/ppermute | solution.py:28
  6.4 34.0 %collective-permute-start.12 = (bf16[1024,256]{1,0:T(8,128)(2,1)S(1)}, bf16[1024,256]{1,0:T(8,128)(2,1)S(1)}, u32[]{:S(2)}, u32[]{:S(2)}) collective-permute-start(bf16[1024,256]{1,0:T(8,128)(2,1)S(1)} %get-tuple-element.60.refs_0_), channel_id=1, source_target_pairs={{0,6},{1,7},{2,4},{3,5},{4,2},{5,3},{6,0},{7,1},{8,14},{9,15},{10,... | collective-permute-start | bytes 1572872 | tf_op jit(solution)/shard_map/ppermute | solution.py:28
  7.9 43.7 %collective-permute-start.10 = (bf16[1024,256]{1,0:T(8,128)(2,1)S(1)}, bf16[1024,256]{1,0:T(8,128)(2,1)}, u32[]{:S(2)}, u32[]{:S(2)}) collective-permute-start(bf16[1024,256]{1,0:T(8,128)(2,1)S(1)} %get-tuple-element.60.refs_0_), channel_id=1, source_target_pairs={{0,4},{1,5},{2,6},{3,7},{4,0},{5,1},{6,2},{7,3},{8,12},{9,13},{10,... | collective-permute-start | bytes 1572872 | tf_op jit(solution)/shard_map/ppermute | solution.py:28
  8.0 43.6 %collective-permute-start.8 = (bf16[1024,256]{1,0:T(8,128)(2,1)S(1)}, bf16[1024,256]{1,0:T(8,128)(2,1)}, u32[]{:S(2)}, u32[]{:S(2)}) collective-permute-start(bf16[1024,256]{1,0:T(8,128)(2,1)S(1)} %get-tuple-element.60.refs_0_), channel_id=1, source_target_pairs={{0,2},{1,3},{2,0},{3,1},{4,6},{5,7},{6,4},{7,5},{8,10},{9,11},{10,... | collective-permute-start | bytes 1572872 | tf_op jit(solution)/shard_map/ppermute | solution.py:28
  18.8 68.8 %collective-permute-start = (bf16[1024,256]{1,0:T(8,128)(2,1)S(1)}, bf16[1024,256]{1,0:T(8,128)(2,1)S(1)}, u32[]{:S(2)}, u32[]{:S(2)}) collective-permute-start(bf16[1024,256]{1,0:T(8,128)(2,1)S(1)} %get-tuple-element.16.refs_0_), channel_id=1, source_target_pairs={{0,2},{1,3},{2,0},{3,1},{4,6},{5,7},{6,4},{7,5},{8,10},{9,11},{10,... | collective-permute-start | bytes 1572872 | tf_op jit(solution)/shard_map/ppermute | solution.py:28
  40.4 47.2 %collective-permute-start.7 = (bf16[1024,256]{1,0:T(8,128)(2,1)S(1)}, bf16[1024,256]{1,0:T(8,128)(2,1)}, u32[]{:S(2)}, u32[]{:S(2)}) collective-permute-start(bf16[1024,256]{1,0:T(8,128)(2,1)S(1)} %get-tuple-element.60.refs_0_), channel_id=1, source_target_pairs={{0,1},{1,0},{2,3},{3,2},{4,5},{5,4},{6,7},{7,6},{8,9},{9,8},{10,11... | collective-permute-start | bytes 1572872 | tf_op jit(solution)/shard_map/ppermute | solution.py:28
  40.4 47.7 %collective-permute-start.13 = (bf16[1024,256]{1,0:T(8,128)(2,1)S(1)}, bf16[1024,256]{1,0:T(8,128)(2,1)}, u32[]{:S(2)}, u32[]{:S(2)}) collective-permute-start(bf16[1024,256]{1,0:T(8,128)(2,1)S(1)} %collective-permute-done.12.refs_6_), channel_id=1, source_target_pairs={{0,1},{1,0},{2,3},{3,2},{4,5},{5,4},{6,7},{7,6},{8,9},{9,8},{10,11... | collective-permute-start | bytes 1572872 | tf_op jit(solution)/shard_map/ppermute | solution.py:28
  51.6 36.5 %collective-permute-start.11 = (bf16[1024,256]{1,0:T(8,128)(2,1)}, bf16[1024,256]{1,0:T(8,128)(2,1)}, u32[]{:S(2)}, u32[]{:S(2)}) collective-permute-start(bf16[1024,256]{1,0:T(8,128)(2,1)} %collective-permute-done.10.refs_4_), channel_id=1, source_target_pairs={{0,1},{1,0},{2,3},{3,2},{4,5},{5,4},{6,7},{7,6},{8,9},{9,8},{10,11... | collective-permute-start | bytes 1572872 | tf_op jit(solution)/shard_map/ppermute | solution.py:28
  51.6 37.0 %collective-permute-start.9 = (bf16[1024,256]{1,0:T(8,128)(2,1)}, bf16[1024,256]{1,0:T(8,128)(2,1)}, u32[]{:S(2)}, u32[]{:S(2)}) collective-permute-start(bf16[1024,256]{1,0:T(8,128)(2,1)} %collective-permute-done.8.refs_2_), channel_id=1, source_target_pairs={{0,1},{1,0},{2,3},{3,2},{4,5},{5,4},{6,7},{7,6},{8,9},{9,8},{10,11... | collective-permute-start | bytes 1572872 | tf_op jit(solution)/shard_map/ppermute | solution.py:28
  87.6 12.7 %collective-permute-start.3 = (bf16[1024,256]{1,0:T(8,128)(2,1)S(1)}, bf16[1024,256]{1,0:T(8,128)(2,1)S(1)}, u32[]{:S(2)}, u32[]{:S(2)}) collective-permute-start(bf16[1024,256]{1,0:T(8,128)(2,1)S(1)} %get-tuple-element.16.refs_0_), channel_id=1, source_target_pairs={{0,1},{1,0},{2,3},{3,2},{4,5},{5,4},{6,7},{7,6},{8,9},{9,8},{10,11... | collective-permute-start | bytes 1572872 | tf_op jit(solution)/shard_map/ppermute | solution.py:28
  87.6 12.7 %collective-permute-start.4 = (bf16[1024,256]{1,0:T(8,128)(2,1)S(1)}, bf16[1024,256]{1,0:T(8,128)(2,1)S(1)}, u32[]{:S(2)}, u32[]{:S(2)}) collective-permute-start(bf16[1024,256]{1,0:T(8,128)(2,1)S(1)} %collective-permute-done.refs_2_), channel_id=1, source_target_pairs={{0,1},{1,0},{2,3},{3,2},{4,5},{5,4},{6,7},{7,6},{8,9},{9,8},{10,11... | collective-permute-start | bytes 1572872 | tf_op jit(solution)/shard_map/ppermute | solution.py:28
  88.1 12.2 %collective-permute-start.5 = (bf16[1024,256]{1,0:T(8,128)(2,1)S(1)}, bf16[1024,256]{1,0:T(8,128)(2,1)S(1)}, u32[]{:S(2)}, u32[]{:S(2)}) collective-permute-start(bf16[1024,256]{1,0:T(8,128)(2,1)S(1)} %collective-permute-done.1.refs_4_), channel_id=1, source_target_pairs={{0,1},{1,0},{2,3},{3,2},{4,5},{5,4},{6,7},{7,6},{8,9},{9,8},{10,11... | collective-permute-start | bytes 1572872 | tf_op jit(solution)/shard_map/ppermute | solution.py:28
  88.2 12.1 %collective-permute-start.6 = (bf16[1024,256]{1,0:T(8,128)(2,1)S(1)}, bf16[1024,256]{1,0:T(8,128)(2,1)S(1)}, u32[]{:S(2)}, u32[]{:S(2)}) collective-permute-start(bf16[1024,256]{1,0:T(8,128)(2,1)S(1)} %collective-permute-done.2.refs_6_), channel_id=1, source_target_pairs={{0,1},{1,0},{2,3},{3,2},{4,5},{5,4},{6,7},{7,6},{8,9},{9,8},{10,11... | collective-permute-start | bytes 1572872 | tf_op jit(solution)/shard_map/ppermute | solution.py:28
  173.5 14.9 %collective-permute-start.26 = (bf16[1024,256]{1,0:T(8,128)(2,1)S(1)}, bf16[1024,256]{1,0:T(8,128)(2,1)S(1)}, u32[]{:S(2)}, u32[]{:S(2)}) collective-permute-start(bf16[1024,256]{1,0:T(8,128)(2,1)S(1)} %dynamic-slice_convert_fusion.7), channel_id=1, source_target_pairs={{0,2},{1,3},{2,0},{3,1},{4,6},{5,7},{6,4},{7,5},{8,10},{9,11},{10,... | collective-permute-start | bytes 1572872 | tf_op jit(solution)/shard_map/ppermute | solution.py:28
  174.2 15.0 %collective-permute-start.28 = (bf16[1024,256]{1,0:T(8,128)(2,1)S(1)}, bf16[1024,256]{1,0:T(8,128)(2,1)S(1)}, u32[]{:S(2)}, u32[]{:S(2)}) collective-permute-start(bf16[1024,256]{1,0:T(8,128)(2,1)S(1)} %dynamic-slice_convert_fusion.6), channel_id=1, source_target_pairs={{0,4},{1,5},{2,6},{3,7},{4,0},{5,1},{6,2},{7,3},{8,12},{9,13},{10,... | collective-permute-start | bytes 1572872 | tf_op jit(solution)/shard_map/ppermute | solution.py:28
  178.1 21.5 %collective-permute-start.42 = (bf16[1024,256]{1,0:T(8,128)(2,1)S(1)}, bf16[1024,256]{1,0:T(8,128)(2,1)S(1)}, u32[]{:S(2)}, u32[]{:S(2)}) collective-permute-start(bf16[1024,256]{1,0:T(8,128)(2,1)S(1)} %dynamic-slice_convert_fusion.5), channel_id=1, source_target_pairs={{0,2},{1,3},{2,0},{3,1},{4,6},{5,7},{6,4},{7,5},{8,10},{9,11},{10,... | collective-permute-start | bytes 1572872 | tf_op jit(solution)/shard_map/ppermute | solution.py:28
  178.8 21.6 %collective-permute-start.44 = (bf16[1024,256]{1,0:T(8,128)(2,1)S(1)}, bf16[1024,256]{1,0:T(8,128)(2,1)S(1)}, u32[]{:S(2)}, u32[]{:S(2)}) collective-permute-start(bf16[1024,256]{1,0:T(8,128)(2,1)S(1)} %dynamic-slice_convert_fusion.4), channel_id=1, source_target_pairs={{0,4},{1,5},{2,6},{3,7},{4,0},{5,1},{6,2},{7,3},{8,12},{9,13},{10,... | collective-permute-start | bytes 1572872 | tf_op jit(solution)/shard_map/ppermute | solution.py:28
  188.5 17.4 %collective-permute-start.27 = (bf16[512,256]{1,0:T(8,128)(2,1)S(1)}, bf16[512,256]{1,0:T(8,128)(2,1)S(1)}, u32[]{:S(2)}, u32[]{:S(2)}) collective-permute-start(bf16[512,256]{1,0:T(8,128)(2,1)S(1)} %dynamic-slice_convert_fusion.15), channel_id=1, source_target_pairs={{0,4},{1,5},{2,6},{3,7},{4,0},{5,1},{6,2},{7,3},{8,12},{9,13},{10,... | collective-permute-start | bytes 786440 | tf_op jit(solution)/shard_map/ppermute | solution.py:28
  189.3 16.6 %collective-permute-start.29 = (bf16[512,256]{1,0:T(8,128)(2,1)S(1)}, bf16[512,256]{1,0:T(8,128)(2,1)S(1)}, u32[]{:S(2)}, u32[]{:S(2)}) collective-permute-start(bf16[512,256]{1,0:T(8,128)(2,1)S(1)} %dynamic-slice_convert_fusion.14), channel_id=1, source_target_pairs={{0,2},{1,3},{2,0},{3,1},{4,6},{5,7},{6,4},{7,5},{8,10},{9,11},{10,... | collective-permute-start | bytes 786440 | tf_op jit(solution)/shard_map/ppermute | solution.py:28
  200.5 22.6 %collective-permute-start.45 = (bf16[512,256]{1,0:T(8,128)(2,1)S(1)}, bf16[512,256]{1,0:T(8,128)(2,1)S(1)}, u32[]{:S(2)}, u32[]{:S(2)}) collective-permute-start(bf16[512,256]{1,0:T(8,128)(2,1)S(1)} %dynamic-slice_convert_fusion.12), channel_id=1, source_target_pairs={{0,2},{1,3},{2,0},{3,1},{4,6},{5,7},{6,4},{7,5},{8,10},{9,11},{10,... | collective-permute-start | bytes 786440 | tf_op jit(solution)/shard_map/ppermute | solution.py:28
  207.2 11.4 %collective-permute-start.31 = (bf16[2,128,256]{2,1,0:T(8,128)(2,1)S(1)}, bf16[2,128,256]{2,1,0:T(8,128)(2,1)S(1)}, u32[]{:S(2)}, u32[]{:S(2)}) collective-permute-start(bf16[2,128,256]{2,1,0:T(8,128)(2,1)S(1)} %get-tuple-element.58), channel_id=1, source_target_pairs={{0,16},{8,24},{16,0},{24,8},{1,17},{9,25},{17,1},{25,9},{2,18},{10... | collective-permute-start | bytes 393224 | tf_op jit(solution)/shard_map/ppermute | solution.py:28
  220.7 13.0 %collective-permute-start.34 = (bf16[2,128,256]{2,1,0:T(8,128)(2,1)S(1)}, bf16[2,128,256]{2,1,0:T(8,128)(2,1)S(1)}, u32[]{:S(2)}, u32[]{:S(2)}) collective-permute-start(bf16[2,128,256]{2,1,0:T(8,128)(2,1)S(1)} %fusion.39), channel_id=1, source_target_pairs={{0,16},{8,24},{16,0},{24,8},{1,17},{9,25},{17,1},{25,9},{2,18},{10... | collective-permute-start | bytes 393224 | tf_op jit(solution)/shard_map/ppermute | solution.py:28
  221.5 12.2 %collective-permute-start.33 = (bf16[2,128,256]{2,1,0:T(8,128)(2,1)S(1)}, bf16[2,128,256]{2,1,0:T(8,128)(2,1)S(1)}, u32[]{:S(2)}, u32[]{:S(2)}) collective-permute-start(bf16[2,128,256]{2,1,0:T(8,128)(2,1)S(1)} %fusion.39), channel_id=1, source_target_pairs={{0,24},{8,16},{16,8},{24,0},{1,25},{9,17},{17,9},{25,1},{2,26},{10... | collective-permute-start | bytes 393224 | tf_op jit(solution)/shard_map/ppermute | solution.py:28
  223.3 12.6 %collective-permute-start.46 = (bf16[2,128,256]{2,1,0:T(8,128)(2,1)S(1)}, bf16[2,128,256]{2,1,0:T(8,128)(2,1)S(1)}, u32[]{:S(2)}, u32[]{:S(2)}) collective-permute-start(bf16[2,128,256]{2,1,0:T(8,128)(2,1)S(1)} %get-tuple-element.50), channel_id=1, source_target_pairs={{0,8},{8,0},{16,24},{24,16},{1,9},{9,1},{17,25},{25,17},{2,10},{10... | collective-permute-start | bytes 393224 | tf_op jit(solution)/shard_map/ppermute | solution.py:28
  224.4 18.8 %collective-permute-start.47 = (bf16[2,128,256]{2,1,0:T(8,128)(2,1)S(1)}, bf16[2,128,256]{2,1,0:T(8,128)(2,1)S(1)}, u32[]{:S(2)}, u32[]{:S(2)}) collective-permute-start(bf16[2,128,256]{2,1,0:T(8,128)(2,1)S(1)} %get-tuple-element.51), channel_id=1, source_target_pairs={{0,16},{8,24},{16,0},{24,8},{1,17},{9,25},{17,1},{25,9},{2,18},{10... | collective-permute-start | bytes 393224 | tf_op jit(solution)/shard_map/ppermute | solution.py:28
  227.9 15.3 %collective-permute-start.48 = (bf16[2,128,256]{2,1,0:T(8,128)(2,1)S(1)}, bf16[2,128,256]{2,1,0:T(8,128)(2,1)S(1)}, u32[]{:S(2)}, u32[]{:S(2)}) collective-permute-start(bf16[2,128,256]{2,1,0:T(8,128)(2,1)S(1)} %get-tuple-element.52), channel_id=1, source_target_pairs={{0,24},{8,16},{16,8},{24,0},{1,25},{9,17},{17,9},{25,1},{2,26},{10... | collective-permute-start | bytes 393224 | tf_op jit(solution)/shard_map/ppermute | solution.py:28
  233.8 14.1 %collective-permute-start.36 = (bf16[512,256]{1,0:T(8,128)(2,1)S(1)}, bf16[512,256]{1,0:T(8,128)(2,1)S(1)}, u32[]{:S(2)}, u32[]{:S(2)}) collective-permute-start(bf16[512,256]{1,0:T(8,128)(2,1)S(1)} %get-tuple-element.82), channel_id=1, source_target_pairs={{0,4},{1,5},{2,6},{3,7},{4,0},{5,1},{6,2},{7,3},{8,12},{9,13},{10,... | collective-permute-start | bytes 786440 | tf_op jit(solution)/shard_map/ppermute | solution.py:28
  235.4 12.6 %collective-permute-start.38 = (bf16[512,256]{1,0:T(8,128)(2,1)S(1)}, bf16[512,256]{1,0:T(8,128)(2,1)S(1)}, u32[]{:S(2)}, u32[]{:S(2)}) collective-permute-start(bf16[512,256]{1,0:T(8,128)(2,1)S(1)} %get-tuple-element.83), channel_id=1, source_target_pairs={{0,2},{1,3},{2,0},{3,1},{4,6},{5,7},{6,4},{7,5},{8,10},{9,11},{10,... | collective-permute-start | bytes 786440 | tf_op jit(solution)/shard_map/ppermute | solution.py:28
  245.5 11.7 %collective-permute-start.50 = (bf16[2,128,256]{2,1,0:T(8,128)(2,1)S(1)}, bf16[2,128,256]{2,1,0:T(8,128)(2,1)S(1)}, u32[]{:S(2)}, u32[]{:S(2)}) collective-permute-start(bf16[2,128,256]{2,1,0:T(8,128)(2,1)S(1)} %fusion.29), channel_id=1, source_target_pairs={{0,16},{8,24},{16,0},{24,8},{1,17},{9,25},{17,1},{25,9},{2,18},{10... | collective-permute-start | bytes 393224 | tf_op jit(solution)/shard_map/ppermute | solution.py:28
  248.1 14.6 %collective-permute-start.39 = (bf16[1024,256]{1,0:T(8,128)(2,1)S(1)}, bf16[1024,256]{1,0:T(8,128)(2,1)S(1)}, u32[]{:S(2)}, u32[]{:S(2)}) collective-permute-start(bf16[1024,256]{1,0:T(8,128)(2,1)S(1)} %pad_maximum_fusion.6), channel_id=1, source_target_pairs={{0,4},{1,5},{2,6},{3,7},{4,0},{5,1},{6,2},{7,3},{8,12},{9,13},{10,... | collective-permute-start | bytes 1572872 | tf_op jit(solution)/shard_map/ppermute | solution.py:28
  257.3 12.5 %collective-permute-start.37 = (bf16[1024,256]{1,0:T(8,128)(2,1)S(1)}, bf16[1024,256]{1,0:T(8,128)(2,1)S(1)}, u32[]{:S(2)}, u32[]{:S(2)}) collective-permute-start(bf16[1024,256]{1,0:T(8,128)(2,1)S(1)} %pad_maximum_fusion.5), channel_id=1, source_target_pairs={{0,2},{1,3},{2,0},{3,1},{4,6},{5,7},{6,4},{7,5},{8,10},{9,11},{10,... | collective-permute-start | bytes 1572872 | tf_op jit(solution)/shard_map/ppermute | solution.py:28
  258.9 11.4 %collective-permute-start.52 = (bf16[512,256]{1,0:T(8,128)(2,1)S(1)}, bf16[512,256]{1,0:T(8,128)(2,1)S(1)}, u32[]{:S(2)}, u32[]{:S(2)}) collective-permute-start(bf16[512,256]{1,0:T(8,128)(2,1)S(1)} %get-tuple-element.74), channel_id=1, source_target_pairs={{0,4},{1,5},{2,6},{3,7},{4,0},{5,1},{6,2},{7,3},{8,12},{9,13},{10,... | collective-permute-start | bytes 786440 | tf_op jit(solution)/shard_map/ppermute | solution.py:28
  259.6 13.1 %collective-permute-start.54 = (bf16[512,256]{1,0:T(8,128)(2,1)S(1)}, bf16[512,256]{1,0:T(8,128)(2,1)S(1)}, u32[]{:S(2)}, u32[]{:S(2)}) collective-permute-start(bf16[512,256]{1,0:T(8,128)(2,1)S(1)} %get-tuple-element.75), channel_id=1, source_target_pairs={{0,2},{1,3},{2,0},{3,1},{4,6},{5,7},{6,4},{7,5},{8,10},{9,11},{10,... | collective-permute-start | bytes 786440 | tf_op jit(solution)/shard_map/ppermute | solution.py:28
  270.2 18.5 %collective-permute-start.40 = (bf16[4096,256]{1,0:T(8,128)(2,1)S(1)}, bf16[4096,256]{1,0:T(8,128)(2,1)S(1)}, u32[]{:S(2)}, u32[]{:S(2)}) collective-permute-start(bf16[4096,256]{1,0:T(8,128)(2,1)S(1)} %pad_maximum_fusion), channel_id=1, source_target_pairs={{0,1},{1,0},{2,3},{3,2},{4,5},{5,4},{6,7},{7,6},{8,9},{9,8},{10,11... | collective-permute-start | bytes 6291464 | tf_op jit(solution)/shard_map/ppermute | solution.py:28
  272.8 13.9 %collective-permute-start.55 = (bf16[1024,256]{1,0:T(8,128)(2,1)S(1)}, bf16[1024,256]{1,0:T(8,128)(2,1)S(1)}, u32[]{:S(2)}, u32[]{:S(2)}) collective-permute-start(bf16[1024,256]{1,0:T(8,128)(2,1)S(1)} %pad_maximum_fusion.9), channel_id=1, source_target_pairs={{0,4},{1,5},{2,6},{3,7},{4,0},{5,1},{6,2},{7,3},{8,12},{9,13},{10,... | collective-permute-start | bytes 1572872 | tf_op jit(solution)/shard_map/ppermute | solution.py:28
  276.6 11.7 %collective-permute-start.53 = (bf16[1024,256]{1,0:T(8,128)(2,1)S(1)}, bf16[1024,256]{1,0:T(8,128)(2,1)S(1)}, u32[]{:S(2)}, u32[]{:S(2)}) collective-permute-start(bf16[1024,256]{1,0:T(8,128)(2,1)S(1)} %pad_maximum_fusion.8), channel_id=1, source_target_pairs={{0,2},{1,3},{2,0},{3,1},{4,6},{5,7},{6,4},{7,5},{8,10},{9,11},{10,... | collective-permute-start | bytes 1572872 | tf_op jit(solution)/shard_map/ppermute | solution.py:28
  377.6 14.9 %collective-permute-start.70 = (bf16[2,1,512,256]{3,2,1,0:T(8,128)(2,1)S(1)}, bf16[2,1,512,256]{3,2,1,0:T(8,128)(2,1)S(1)}, u32[]{:S(2)}, u32[]{:S(2)}) collective-permute-start(bf16[2,1,512,256]{3,2,1,0:T(8,128)(2,1)S(1)} %dynamic-slice_convert_fusion.3), channel_id=1, source_target_pairs={{0,2},{1,3},{2,0},{3,1},{4,6},{5,7},{6,4},{7,5},{8,10},{9,11},{10,... | collective-permute-start | bytes 1572872 | tf_op jit(solution)/shard_map/ppermute | solution.py:28
  379.4 14.9 %collective-permute-start.72 = (bf16[1,2,512,256]{3,2,1,0:T(8,128)(2,1)S(1)}, bf16[1,2,512,256]{3,2,1,0:T(8,128)(2,1)S(1)}, u32[]{:S(2)}, u32[]{:S(2)}) collective-permute-start(bf16[1,2,512,256]{3,2,1,0:T(8,128)(2,1)S(1)} %dynamic-slice_convert_fusion.2), channel_id=1, source_target_pairs={{0,4},{1,5},{2,6},{3,7},{4,0},{5,1},{6,2},{7,3},{8,12},{9,13},{10,... | collective-permute-start | bytes 1572872 | tf_op jit(solution)/shard_map/ppermute | solution.py:28
  385.2 18.5 %collective-permute-start.77 = (bf16[2,1,512,256]{3,2,1,0:T(8,128)(2,1)S(1)}, bf16[2,1,512,256]{3,2,1,0:T(8,128)(2,1)S(1)}, u32[]{:S(2)}, u32[]{:S(2)}) collective-permute-start(bf16[2,1,512,256]{3,2,1,0:T(8,128)(2,1)S(1)} %dynamic-slice_convert_fusion.1), channel_id=1, source_target_pairs={{0,2},{1,3},{2,0},{3,1},{4,6},{5,7},{6,4},{7,5},{8,10},{9,11},{10,... | collective-permute-start | bytes 1572872 | tf_op jit(solution)/shard_map/ppermute | solution.py:28
  386.7 18.8 %collective-permute-start.79 = (bf16[1,2,512,256]{3,2,1,0:T(8,128)(2,1)S(1)}, bf16[1,2,512,256]{3,2,1,0:T(8,128)(2,1)S(1)}, u32[]{:S(2)}, u32[]{:S(2)}) collective-permute-start(bf16[1,2,512,256]{3,2,1,0:T(8,128)(2,1)S(1)} %dynamic-slice_convert_fusion), channel_id=1, source_target_pairs={{0,4},{1,5},{2,6},{3,7},{4,0},{5,1},{6,2},{7,3},{8,12},{9,13},{10,... | collective-permute-start | bytes 1572872 | tf_op jit(solution)/shard_map/ppermute | solution.py:28
  392.6 18.5 %collective-permute-start.71 = (bf16[1,512,256]{2,1,0:T(8,128)(2,1)S(1)}, bf16[1,512,256]{2,1,0:T(8,128)(2,1)S(1)}, u32[]{:S(2)}, u32[]{:S(2)}) collective-permute-start(bf16[1,512,256]{2,1,0:T(8,128)(2,1)S(1)} %fusion.14), channel_id=1, source_target_pairs={{0,4},{1,5},{2,6},{3,7},{4,0},{5,1},{6,2},{7,3},{8,12},{9,13},{10,... | collective-permute-start | bytes 786440 | tf_op jit(solution)/shard_map/ppermute | solution.py:28
  394.4 16.8 %collective-permute-start.73 = (bf16[1,512,256]{2,1,0:T(8,128)(2,1)S(1)}, bf16[1,512,256]{2,1,0:T(8,128)(2,1)S(1)}, u32[]{:S(2)}, u32[]{:S(2)}) collective-permute-start(bf16[1,512,256]{2,1,0:T(8,128)(2,1)S(1)} %fusion.15), channel_id=1, source_target_pairs={{0,2},{1,3},{2,0},{3,1},{4,6},{5,7},{6,4},{7,5},{8,10},{9,11},{10,... | collective-permute-start | bytes 786440 | tf_op jit(solution)/shard_map/ppermute | solution.py:28
  403.9 11.7 %collective-permute-start.78 = (bf16[1,512,256]{2,1,0:T(8,128)(2,1)S(1)}, bf16[1,512,256]{2,1,0:T(8,128)(2,1)S(1)}, u32[]{:S(2)}, u32[]{:S(2)}) collective-permute-start(bf16[1,512,256]{2,1,0:T(8,128)(2,1)S(1)} %fusion.16), channel_id=1, source_target_pairs={{0,4},{1,5},{2,6},{3,7},{4,0},{5,1},{6,2},{7,3},{8,12},{9,13},{10,... | collective-permute-start | bytes 786440 | tf_op jit(solution)/shard_map/ppermute | solution.py:28
  413.1 18.8 %collective-permute-start.75 = (bf16[64,1024]{1,0:T(8,128)(2,1)S(1)}, bf16[64,1024]{1,0:T(8,128)(2,1)S(1)}, u32[]{:S(2)}, u32[]{:S(2)}) collective-permute-start(bf16[64,1024]{1,0:T(8,128)(2,1)S(1)} %get-tuple-element.42), channel_id=1, source_target_pairs={{0,16},{8,24},{16,0},{24,8},{1,17},{9,25},{17,1},{25,9},{2,18},{10... | collective-permute-start | bytes 393224 | tf_op jit(solution)/shard_map/ppermute | solution.py:28
  416.2 15.9 %collective-permute-start.81 = (bf16[64,1024]{1,0:T(8,128)(2,1)S(1)}, bf16[64,1024]{1,0:T(8,128)(2,1)S(1)}, u32[]{:S(2)}, u32[]{:S(2)}) collective-permute-start(bf16[64,1024]{1,0:T(8,128)(2,1)S(1)} %get-tuple-element.43), channel_id=1, source_target_pairs={{0,8},{8,0},{16,24},{24,16},{1,9},{9,1},{17,25},{25,17},{2,10},{10... | collective-permute-start | bytes 393224 | tf_op jit(solution)/shard_map/ppermute | solution.py:28
  416.8 15.2 %collective-permute-start.83 = (bf16[64,1024]{1,0:T(8,128)(2,1)S(1)}, bf16[64,1024]{1,0:T(8,128)(2,1)S(1)}, u32[]{:S(2)}, u32[]{:S(2)}) collective-permute-start(bf16[64,1024]{1,0:T(8,128)(2,1)S(1)} %get-tuple-element.44), channel_id=1, source_target_pairs={{0,24},{8,16},{16,8},{24,0},{1,25},{9,17},{17,9},{25,1},{2,26},{10... | collective-permute-start | bytes 393224 | tf_op jit(solution)/shard_map/ppermute | solution.py:28
  418.1 17.7 %collective-permute-start.82 = (bf16[64,1024]{1,0:T(8,128)(2,1)S(1)}, bf16[64,1024]{1,0:T(8,128)(2,1)S(1)}, u32[]{:S(2)}, u32[]{:S(2)}) collective-permute-start(bf16[64,1024]{1,0:T(8,128)(2,1)S(1)} %get-tuple-element.45), channel_id=1, source_target_pairs={{0,16},{8,24},{16,0},{24,8},{1,17},{9,25},{17,1},{25,9},{2,18},{10... | collective-permute-start | bytes 393224 | tf_op jit(solution)/shard_map/ppermute | solution.py:28
  (56 other events, 388.1 us)
